TPU v7x, 32 devices: a whole 2x2x4 slice. The times are simulated.
32 devices in a mesh: grp: 4 (over z), dev: 8 (over y, x, core).
Axes of the slice: x: 2, y: 2, z: 4, core: 2. Of those that a mesh axis runs over, the one named last changes fastest.
Arguments:
- stamps: int32 [65536], P(('grp', 'dev')), may hold values from 0 to 14399, as said below
- account: int32 [65536], P(('grp', 'dev')), may hold values from 0 to 15, as said below
- kind: int32 [65536], P(('grp', 'dev')), may hold values from 0 to 5
- weight: bfloat16 [65536], P(('grp', 'dev')), may hold values from -3 to 3
- used: int32 [32, 64], P(('grp', 'dev')), may hold values from 1 to 32, as said below
Outputs:
- pair_profile: float32 [36, 1024], P(None, 'dev')
- triple_profile: float32 [8, 1024], P(None, 'dev')
Inputs may be any that keep to these rules, and one draw needn't show every extreme that they name: `account`: small values are more common. `stamps`: an event of sender r lies in time range r // 8: its stamp is at least (r // 8) * 3600 and below that plus 3600. `used`: column 0 of every row equals 32.
All inputs are finite; a program needn't handle non-finite values.
Results may differ from a plain program's by a relative error of at most 0.0003.
Values sent between devices are 32-bit elements; how exact they have to be, the bound alone decides.
A program may use at most 64 MiB of HBM per device.

v0:
```python
import math

import jax
import jax.numpy as jnp
from jax import lax
from jax.sharding import PartitionSpec as P

DELTA = 3600
ACC_BLK = 16


def passed_along(block, axis, distance):
    devices = range(lax.axis_size(axis))
    route = [(i - distance, i) for i in devices if i - distance in devices]
    return lax.ppermute(block, axis, route)


def count_block(own_rows, prior_rows):
    fields = jnp.concatenate([prior_rows, own_rows], axis=1)
    stamp, local, kinds, wt = (fields[0], fields[1], fields[2], fields[3])
    blk = own_rows.shape[1]
    gap = stamp[None, :] - stamp[:, None]
    linked = (local[:, None] == local[None, :]) & (gap > 0.0) & (gap <= DELTA)
    link_all = linked.astype(jnp.bfloat16)
    link_own = link_all[:, blk:]
    classes = (kinds[:, None] == jnp.arange(6).astype(jnp.float32)[None, :]).astype(
        jnp.float32
    ) * wt[:, None]
    earlier = jnp.einsum(
        "ik,ic->kc", link_own, classes.astype(jnp.bfloat16), preferred_element_type=jnp.float32
    )
    later = classes[blk:]
    pair_terms = (earlier[:, :, None] * later[:, None, :]).reshape(blk, 36)
    owners_hot = (local[blk:, None] == jnp.arange(ACC_BLK).astype(jnp.float32)[None, :]).astype(
        jnp.float32
    )
    pairs = jnp.dot(pair_terms.T, owners_hot, precision=lax.Precision.HIGHEST)
    dirs = jnp.stack([wt * (kinds < 2.5), wt * (kinds > 2.5)], axis=0)
    weighted = (link_all[None, :, :] * dirs.astype(jnp.bfloat16)[:, None, :]).reshape(
        2 * 2 * blk, 2 * blk
    )
    middle = jnp.dot(weighted, link_own, preferred_element_type=jnp.float32).reshape(
        2, 2 * blk, blk
    )
    closed = middle * link_own.astype(jnp.float32)[None]
    ends = jnp.einsum("ai,bik->abk", dirs, closed, precision=lax.Precision.HIGHEST)
    last = dirs[:, blk:]
    triple_terms = (ends[:, :, None, :] * last[None, None, :, :]).reshape(8, blk)
    triples = jnp.dot(triple_terms, owners_hot, precision=lax.Precision.HIGHEST)
    return (pairs, triples)


def per_device(stamps, account, kind, weight, used):
    owners = lax.axis_size("dev")
    blocks = used.shape[1] // owners
    slots = stamps.shape[0] // (owners * blocks)
    shape3 = (owners, blocks, slots)
    live = used.reshape(owners, blocks, 1) > jnp.arange(slots)
    wt = jnp.where(live, weight.reshape(shape3).astype(jnp.float32), jnp.float32(0.0))
    stacked = jnp.stack(
        [
            stamps.reshape(shape3).astype(jnp.float32),
            account.reshape(shape3).astype(jnp.float32),
            kind.reshape(shape3).astype(jnp.float32),
            wt,
        ],
        axis=2,
    )
    own_events = lax.all_to_all(stacked, "dev", split_axis=0, concat_axis=3, tiled=True)[0]
    prior_events = passed_along(own_events, "grp", 1)
    width = own_events.shape[2]
    batch = math.gcd(blocks, 16)
    own_b = own_events.reshape(blocks // batch, batch, 4, width)
    prior_b = prior_events.reshape(blocks // batch, batch, 4, width)
    pairs, triples = lax.map(lambda xs: jax.vmap(count_block)(xs[0], xs[1]), (own_b, prior_b))
    pairs = pairs.reshape(blocks, 36, ACC_BLK).transpose(1, 0, 2).reshape(36, blocks * ACC_BLK)
    triples = triples.reshape(blocks, 8, ACC_BLK).transpose(1, 0, 2).reshape(8, blocks * ACC_BLK)
    pair_profile, triple_profile = lax.psum((pairs, triples), "grp")
    return (pair_profile, triple_profile)


def solution(mesh):
    return jax.shard_map(
        per_device,
        mesh=mesh,
        in_specs=(
            P(("grp", "dev")),
            P(("grp", "dev")),
            P(("grp", "dev")),
            P(("grp", "dev")),
            P(("grp", "dev"), None),
        ),
        out_specs=(P(None, "dev"), P(None, "dev")),
        check_vma=False,
    )
```

profile of v0, /device:TPU:0, one launch (start us, length us, event | category | flops | bytes accessed | tf_op | source)
XLA Modules:
  0.0 68.0 jit_solution(14284475883361899164)
XLA Ops:
  0.6 0.5 broadcast.127
  1.1 1.3 %reduce.3 = s32[64]{0:T(128)S(1)} reduce(s32[1,64]{1,0:T(1,128)} %param.9, s32[]{:T(128)} %broadcast.127), dimensions={0}, to_apply=%param.9.reduce_sub_computation.3 | reduce | bytes 516 | tf_op args[4]
  2.5 0.1 gt.42
  2.5 0.7 %convert_element_type.96 = f32[2048]{0:T(1024)S(1)} convert(s32[2048]{0:T(1024)} %param.5) | non-fusion elementwise | flops 2048 | bytes 16384 | tf_op jit(solution)/shard_map/convert_element_type | solution.py:62
  3.2 0.7 %convert_element_type.98 = f32[2048]{0:T(1024)S(1)} convert(s32[2048]{0:T(1024)} %param.6) | non-fusion elementwise | flops 2048 | bytes 16384 | tf_op jit(solution)/shard_map/convert_element_type | solution.py:63
  3.9 0.7 %convert_element_type.100 = f32[2048]{0:T(1024)S(1)} convert(s32[2048]{0:T(1024)} %param.7) | non-fusion elementwise | flops 2048 | bytes 16384 | tf_op jit(solution)/shard_map/convert_element_type | solution.py:64
  4.6 0.1 convert_element_type.101
  4.8 0.1 convert_element_type.97
  4.9 0.8 %reshape.175 = f32[8,8,1,32]{3,1,0,2:T(8,128)S(1)} reshape(bf16[2048]{0:T(1024)(128)(2,1)} %param.8) | data formatting | bytes 12288 | tf_op jit(solution)/shard_map/convert_element_type | solution.py:59
  5.6 0.1 fusion.19
  5.7 0.7 %reshape.186 = f32[8,1,1024]{2,1,0:T(1,128)} reshape(f32[8,4,8,32]{3,2,1,0:T(8,128)S(1)} %copy_bitcast_fusion.4) | data formatting | bytes 65536
  6.5 5.2 %all-to-all-start = ((f32[8,1,1024]{2,1,0:T(1,128)}), f32[8,1,1024]{2,1,0:T(1,128)S(1)}, u32[]{:S(2)}, u32[]{:S(2)}) async-start(f32[8,1,1024]{2,1,0:T(1,128)} %reshape.186), calls=%async_computation | async-start | bytes 65536 | tf_op jit(solution)/shard_map/all_to_all | solution.py:69
  11.7 4.8 %all-to-all-done = f32[8,1,1024]{2,1,0:T(1,128)S(1)} async-done(((f32[8,1,1024]{2,1,0:T(1,128)}), f32[8,1,1024]{2,1,0:T(1,128)S(1)}, u32[]{:S(2)}, u32[]{:S(2)}) %all-to-all-start) | async-done | bytes 32800 | tf_op jit(solution)/shard_map/all_to_all | solution.py:69
  16.5 0.5 broadcast.128
  17.0 0.7 %reduce.4 = f32[8,1024]{1,0:T(8,128)S(1)} reduce(f32[8,1,1024]{2,1,0:T(1,128)S(1)} %all-to-all-done, f32[]{:T(128)} %broadcast.128), dimensions={1}, to_apply=%all_to_all.11.reduce_sub_computation | reduce | bytes 65540 | tf_op jit(solution)/shard_map/all_to_all | solution.py:69
  17.7 0.1 reshape.187
  17.8 0.1 copy.18
  17.9 0.1 squeeze.22
  18.0 3.5 %collective-permute-start = (f32[8,4,256]{2,1,0:T(4,128)S(1)}, f32[8,4,256]{2,1,0:T(4,128)S(1)}, u32[]{:S(2)}, u32[]{:S(2)}) collective-permute-start(f32[8,4,256]{2,1,0:T(4,128)S(1)} %squeeze.22), channel_id=1, source_target_pairs={{0,8},{8,16},{16,24},{1,9},{9,17},{17,25},{2,10},{10,18},{18,26},{... | collective-permute-start | bytes 98312 | tf_op jit(solution)/shard_map/ppermute | solution.py:15
  21.5 1.6 %collective-permute-done = f32[8,4,256]{2,1,0:T(4,128)S(1)} collective-permute-done((f32[8,4,256]{2,1,0:T(4,128)S(1)}, f32[8,4,256]{2,1,0:T(4,128)S(1)}, u32[]{:S(2)}, u32[]{:S(2)}) %collective-permute-start) | collective-permute-done | bytes 32800 | tf_op jit(solution)/shard_map/ppermute | solution.py:15
  23.1 0.1 fusion.23
  23.3 0.1 compare_select_fusion
  23.4 4.1 %fusion.26 = (bf16[8,512,512]{2,1,0:T(8,128)(2,1)}, pred[8,512,512]{2,1,0:T(32,128)(4,1)S(1)}) fusion(f32[8,512]{1,0:T(8,128)S(1)} %get-tuple-element.29, f32[8,512]{1,0:T(8,128)S(1)} %get-tuple-element.30), kind=kLoop, calls=%fused_computation.50 | loop fusion | flops 14680064 | bytes 6324224 | tf_op jit(solution)/shard_map/while/body/eval_jaxpr/vmap()/convert_element_type | solution.py:24
  27.5 0.8 %fusion.7 = f32[8,256,6]{1,2,0:T(8,128)S(1)} fusion(pred[8,512,512]{2,1,0:T(32,128)(4,1)S(1)} %get-tuple-element.26, f32[8,512]{1,0:T(8,128)S(1)} %get-tuple-element.27, f32[8,512]{1,0:T(8,128)S(1)} %get-tuple-element.28, f32[6]{0:T(128)S(1)} %iota_convert_fusion.1), kind=kOutput, calls=%fused_computation.10 | convolution fusion | flops 12632064 | bytes 1131008 | tf_op jit(solution)/shard_map/while/body/eval_jaxpr/vmap(ik,ic->kc)/dot_general | solution.py:29
  28.3 0.3 fusion.9
  28.8 4.1 %slice_convert_fusion = f32[8,512,256]{2,1,0:T(8,128)} fusion(bf16[8,512,512]{2,1,0:T(8,128)(2,1)} %get-tuple-element.25), kind=kLoop, calls=%fused_computation.12 | loop fusion | flops 1048576 | bytes 6291456 | tf_op jit(solution)/shard_map/while/body/eval_jaxpr/vmap()/convert_element_type | solution.py:45
  32.9 3.8 %broadcast_multiply_fusion = bf16[8,2,512,512]{3,2,1,0:T(8,128)(2,1)} fusion(bf16[8,2,512]{2,1,0:T(2,128)(2,1)S(1)} %convert_bitcast_fusion, bf16[8,512,512]{2,1,0:T(8,128)(2,1)S(1)} %copy-done), kind=kLoop, calls=%fused_computation.7 | loop fusion | flops 4194304 | bytes 12599296 | tf_op jit(solution)/shard_map/while/body/eval_jaxpr/vmap()/mul | solution.py:39
  36.7 5.9 %fusion.5 = f32[8,1024,256]{2,1,0:T(8,128)S(1)} fusion(bf16[8,1024,512]{2,1,0:T(8,128)(2,1)} %bitcast.42, pred[8,512,512]{2,1,0:T(32,128)(4,1)S(1)} %get-tuple-element.26), kind=kOutput, calls=%fused_computation.8 | convolution fusion | flops 2147483648 | bytes 17825792 | tf_op jit(solution)/shard_map/while/body/eval_jaxpr/vmap()/dot_general | solution.py:42
  42.6 4.3 %fusion = f32[8,2,2,256]{3,1,2,0:T(2,128)S(1)} fusion(f32[8,2,512,256]{3,2,1,0:T(8,128)S(1)} %bitcast.41, f32[8,512,256]{2,1,0:T(8,128)S(1)} %copy-done.1, f32[1,8,512]{2,0,1:T(1,128)S(1)} %get-tuple-element.14, f32[1,8,512]{2,0,1:T(1,128)S(1)} %get-tuple-element.20), kind=kOutput, calls=%fused_computation.2 | convolution fusion | flops 52436992 | bytes 12648448 | tf_op jit(solution)/shard_map/while/body/eval_jaxpr/vmap(ai,bik->abk)/dot_general | solution.py:46
  47.1 0.2 convolution_bitcast_fusion
  47.3 0.1 reshape.174
  47.4 20.5 %all-reduce = (f32[36,128]{1,0:T(8,128)}, f32[8,128]{1,0:T(8,128)}) all-reduce(f32[36,128]{1,0:T(8,128)S(1)} %copy.22, f32[8,128]{1,0:T(8,128)S(1)} %reshape.174), channel_id=1, replica_groups=mesh['grp'=4,'dev'=8] {'grp'}, use_global_device_ids=true, to_apply=%region_0.1 | all-reduce | flops 5632 | bytes 45056 | tf_op jit(solution)/shard_map/psum | solution.py:78
  (25 shorter events, 0.4 us)
Async XLA Ops:
  6.5 10.0 %all-to-all-start = ((f32[8,1,1024]{2,1,0:T(1,128)}), f32[8,1,1024]{2,1,0:T(1,128)S(1)}, u32[]{:S(2)}, u32[]{:S(2)}) async-start(f32[8,1,1024]{2,1,0:T(1,128)} %reshape.186), calls=%async_computation | async-start | bytes 65536 | tf_op jit(solution)/shard_map/all_to_all | solution.py:69
  18.0 5.1 %collective-permute-start = (f32[8,4,256]{2,1,0:T(4,128)S(1)}, f32[8,4,256]{2,1,0:T(4,128)S(1)}, u32[]{:S(2)}, u32[]{:S(2)}) collective-permute-start(f32[8,4,256]{2,1,0:T(4,128)S(1)} %squeeze.22), channel_id=1, source_target_pairs={{0,8},{8,16},{16,24},{1,9},{9,17},{17,25},{2,10},{10,18},{18,26},{... | collective-permute-start | bytes 98312 | tf_op jit(solution)/shard_map/ppermute | solution.py:15
  28.8 4.1 %copy-start = (bf16[8,512,512]{2,1,0:T(8,128)(2,1)S(1)}, bf16[8,512,512]{2,1,0:T(8,128)(2,1)}, u32[]{:S(2)}) copy-start(bf16[8,512,512]{2,1,0:T(8,128)(2,1)} %get-tuple-element.25) | copy-start | bytes 12582916
  36.7 5.9 %copy-start.1 = (f32[8,512,256]{2,1,0:T(8,128)S(1)}, f32[8,512,256]{2,1,0:T(8,128)}, u32[]{:S(2)}) copy-start(f32[8,512,256]{2,1,0:T(8,128)} %slice_convert_fusion) | copy-start | bytes 12582916
where the time goes:
time: 68.4 us; the launch traced here: 68 us
  blocking collectives  20.5 us (30%)
  other arithmetic  16.5 us (24%)
  matrix products  11.6 us (17%)
  starting transfers between devices  8.68 us (13%)
  waiting for transfers between devices  6.41 us (9%)
  local copies, waits for them, and re-layouts  3.4 us (5%)
  between operations  0.83 us (1%)
    psum x1, blocking collectives, per_device(): pair_profile, triple_profile = lax.psum((pairs, triples), 'grp')  20.5 us
    dot_general x1, matrix products, count_block(): jnp.dot(weighted, link_own, preferred_element_type=jnp.float32)  5.9 us
    all_to_all x1, starting transfers between devices, per_device(): lax.all_to_all(stacked, 'dev', split_axis=0, concat_axis=3, tiled=True)[0]  5.2 us
    all_to_all x1, waiting for transfers between devices, per_device(): lax.all_to_all(stacked, 'dev', split_axis=0, concat_axis=3, tiled=True)[0]  4.84 us
    dot_general x1, matrix products, count_block(): jnp.einsum('ai,bik->abk', dirs, closed, precision=lax.Precision.HIGHEST)  4.33 us
    convert_element_type x1, other arithmetic, count_block(): closed = middle * link_own.astype(jnp.float32)[None]  4.11 us
    convert_element_type x1, other arithmetic, count_block(): link_all = linked.astype(jnp.bfloat16)  4.09 us
    mul x1, other arithmetic, count_block(): link_all[None, :, :] * dirs.astype(jnp.bfloat16)[:, None, :]  3.84 us
  transfers between devices with their start and end apart: 2, of which 2 were waited for; matrix products, arithmetic and copies ran while one was open for 0% of the time, Pallas kernels for 0%

commit v1 on v0

--- a/solution.py
+++ b/solution.py
@@ -13,6 +13,24 @@
     devices = range(lax.axis_size(axis))
     route = [(i - distance, i) for i in devices if i - distance in devices]
     return lax.ppermute(block, axis, route)
+
+
+def summed_over(block, axis):
+    n = lax.axis_size(axis)
+    if n & (n - 1) == 0:
+        step = 1
+        while step < n:
+            block = block + lax.ppermute(block, axis, [(i, i ^ step) for i in range(n)])
+            step *= 2
+        return block
+    parts = [block]
+    moving = block
+    for d in range(1, n):
+        moving = lax.ppermute(moving, axis, [(i, (i + 1) % n) for i in range(n)])
+        parts.append(moving)
+    idx = lax.axis_index(axis)
+    ordered = jnp.stack(parts)[(idx - jnp.arange(n)) % n]
+    return ordered.sum(axis=0)
 
 
 def count_block(own_rows, prior_rows):
@@ -75,8 +93,8 @@
     pairs, triples = lax.map(lambda xs: jax.vmap(count_block)(xs[0], xs[1]), (own_b, prior_b))
     pairs = pairs.reshape(blocks, 36, ACC_BLK).transpose(1, 0, 2).reshape(36, blocks * ACC_BLK)
     triples = triples.reshape(blocks, 8, ACC_BLK).transpose(1, 0, 2).reshape(8, blocks * ACC_BLK)
-    pair_profile, triple_profile = lax.psum((pairs, triples), "grp")
-    return (pair_profile, triple_profile)
+    both = summed_over(jnp.concatenate([pairs, triples], axis=0), "grp")
+    return (both[:36], both[36:])
 
 
 def solution(mesh):

time: 68.4 us -> 58.1 us (0.85)
  blocking collectives: 20.5 us -> 0 us
  starting transfers between devices: 8.68 us -> 14.2 us
  waiting for transfers between devices: 6.41 us -> 10 us
  local copies, waits for them, and re-layouts: 3.4 us -> 4.6 us
    psum x1 -> x0, blocking collectives: 20.5 us -> none  [per_device(): pair_profile, triple_profile = lax.psum((pairs, triples), 'grp')]
    ppermute x0 -> x2, starting transfers between devices: none -> 5.48 us  [summed_over(): block = block + lax.ppermute(block, axis, [(i, i ^ step) for i in range(n)])]
    convert_element_type x1 -> x0, other arithmetic: 4.09 us -> none  [count_block(): link_all = linked.astype(jnp.bfloat16)]
    and x0 -> x1, other arithmetic: none -> 4.08 us  [count_block(): linked = (local[:, None] == local[None, :]) & (gap > 0.0) & (gap <= DELTA)]
    ppermute x0 -> x2, waiting for transfers between devices: none -> 3.61 us  [summed_over(): block = block + lax.ppermute(block, axis, [(i, i ^ step) for i in range(n)])]
    slice x0 -> x2, local copies, waits for them, and re-layouts: none -> 1.21 us  [per_device(): return (both[:36], both[36:])]
  transfers between devices with their start and end apart: 2 -> 4, of which waited for: 2 -> 4; matrix products, arithmetic and copies ran while one was open for 0% -> 0% of each run, Pallas kernels for 0% -> 0%
where the time goes in v1:
time: 58.1 us; the launch traced here: 57.7 us
  other arithmetic  16.5 us (28%)
  starting transfers between devices  14.2 us (24%)
  matrix products  11.6 us (20%)
  waiting for transfers between devices  10 us (17%)
  local copies, waits for them, and re-layouts  4.6 us (8%)
  between operations  0.83 us (1%)
    dot_general x1, matrix products, count_block(): jnp.dot(weighted, link_own, preferred_element_type=jnp.float32)  5.9 us
    ppermute x2, starting transfers between devices, summed_over(): block = block + lax.ppermute(block, axis, [(i, i ^ step) for i in range(n)])  5.48 us
    all_to_all x1, starting transfers between devices, per_device(): lax.all_to_all(stacked, 'dev', split_axis=0, concat_axis=3, tiled=True)[0]  5.2 us
    all_to_all x1, waiting for transfers between devices, per_device(): lax.all_to_all(stacked, 'dev', split_axis=0, concat_axis=3, tiled=True)[0]  4.84 us
    dot_general x1, matrix products, count_block(): jnp.einsum('ai,bik->abk', dirs, closed, precision=lax.Precision.HIGHEST)  4.33 us
    convert_element_type x1, other arithmetic, count_block(): closed = middle * link_own.astype(jnp.float32)[None]  4.09 us
    and x1, other arithmetic, count_block(): linked = (local[:, None] == local[None, :]) & (gap > 0.0) & (gap <= DELTA)  4.08 us
    mul x1, other arithmetic, count_block(): link_all[None, :, :] * dirs.astype(jnp.bfloat16)[:, None, :]  3.85 us
  transfers between devices with their start and end apart: 4, of which 4 were waited for; matrix products, arithmetic and copies ran while one was open for 0% of the time, Pallas kernels for 0%

profile of v1, /device:TPU:0, one launch (start us, length us, event | category | flops | bytes accessed | tf_op | source)
XLA Modules:
  0.0 57.7 jit_solution(18139149272456394451)
XLA Ops:
  0.6 0.5 broadcast.127
  1.1 1.3 %reduce.3 = s32[64]{0:T(128)S(1)} reduce(s32[1,64]{1,0:T(1,128)} %param.9, s32[]{:T(128)} %broadcast.127), dimensions={0}, to_apply=%param.9.reduce_sub_computation.3 | reduce | bytes 516 | tf_op args[4]
  2.5 0.1 gt.42
  2.5 0.7 %convert_element_type.96 = f32[2048]{0:T(1024)S(1)} convert(s32[2048]{0:T(1024)} %param.5) | non-fusion elementwise | flops 2048 | bytes 16384 | tf_op jit(solution)/shard_map/convert_element_type | solution.py:80
  3.2 0.7 %convert_element_type.98 = f32[2048]{0:T(1024)S(1)} convert(s32[2048]{0:T(1024)} %param.6) | non-fusion elementwise | flops 2048 | bytes 16384 | tf_op jit(solution)/shard_map/convert_element_type | solution.py:81
  3.9 0.7 %convert_element_type.100 = f32[2048]{0:T(1024)S(1)} convert(s32[2048]{0:T(1024)} %param.7) | non-fusion elementwise | flops 2048 | bytes 16384 | tf_op jit(solution)/shard_map/convert_element_type | solution.py:82
  4.9 0.8 %reshape.175 = f32[8,8,1,32]{3,1,0,2:T(8,128)S(1)} reshape(bf16[2048]{0:T(1024)(128)(2,1)} %param.8) | data formatting | bytes 12288 | tf_op jit(solution)/shard_map/convert_element_type | solution.py:77
  5.7 0.7 %reshape.186 = f32[8,1,1024]{2,1,0:T(1,128)} reshape(f32[8,4,8,32]{3,2,1,0:T(8,128)S(1)} %copy_bitcast_fusion.4) | data formatting | bytes 65536
  6.4 5.2 %all-to-all-start = ((f32[8,1,1024]{2,1,0:T(1,128)}), f32[8,1,1024]{2,1,0:T(1,128)S(1)}, u32[]{:S(2)}, u32[]{:S(2)}) async-start(f32[8,1,1024]{2,1,0:T(1,128)} %reshape.186), calls=%async_computation | async-start | bytes 65536 | tf_op jit(solution)/shard_map/all_to_all | solution.py:87
  11.7 4.8 %all-to-all-done = f32[8,1,1024]{2,1,0:T(1,128)S(1)} async-done(((f32[8,1,1024]{2,1,0:T(1,128)}), f32[8,1,1024]{2,1,0:T(1,128)S(1)}, u32[]{:S(2)}, u32[]{:S(2)}) %all-to-all-start) | async-done | bytes 32800 | tf_op jit(solution)/shard_map/all_to_all | solution.py:87
  16.5 0.5 broadcast.128
  17.0 0.7 %reduce.4 = f32[8,1024]{1,0:T(8,128)S(1)} reduce(f32[8,1,1024]{2,1,0:T(1,128)S(1)} %all-to-all-done, f32[]{:T(128)} %broadcast.128), dimensions={1}, to_apply=%all_to_all.11.reduce_sub_computation | reduce | bytes 65540 | tf_op jit(solution)/shard_map/all_to_all | solution.py:87
  17.7 0.1 reshape.187
  17.8 0.1 copy.18
  17.9 0.1 squeeze.22
  18.0 3.5 %collective-permute-start = (f32[8,4,256]{2,1,0:T(4,128)S(1)}, f32[8,4,256]{2,1,0:T(4,128)S(1)}, u32[]{:S(2)}, u32[]{:S(2)}) collective-permute-start(f32[8,4,256]{2,1,0:T(4,128)S(1)} %squeeze.22), channel_id=1, source_target_pairs={{0,8},{8,16},{16,24},{1,9},{9,17},{17,25},{2,10},{10,18},{18,26},{... | collective-permute-start | bytes 98312 | tf_op jit(solution)/shard_map/ppermute | solution.py:15
  21.5 1.6 %collective-permute-done = f32[8,4,256]{2,1,0:T(4,128)S(1)} collective-permute-done((f32[8,4,256]{2,1,0:T(4,128)S(1)}, f32[8,4,256]{2,1,0:T(4,128)S(1)}, u32[]{:S(2)}, u32[]{:S(2)}) %collective-permute-start) | collective-permute-done | bytes 32800 | tf_op jit(solution)/shard_map/ppermute | solution.py:15
  23.3 0.1 compare_select_fusion
  23.4 4.1 %fusion.3 = (pred[8,512,512]{2,1,0:T(32,128)(4,1)S(1)}, bf16[8,512,512]{2,1,0:T(8,128)(2,1)}) fusion(f32[8,512]{1,0:T(8,128)S(1)} %get-tuple-element.27, f32[8,512]{1,0:T(8,128)S(1)} %get-tuple-element.28), kind=kLoop, calls=%fused_computation.5 | loop fusion | flops 14680064 | bytes 6324224 | tf_op jit(solution)/shard_map/while/body/eval_jaxpr/vmap()/and | solution.py:41
  27.5 0.8 %fusion.7 = f32[8,256,6]{1,2,0:T(8,128)S(1)} fusion(pred[8,512,512]{2,1,0:T(32,128)(4,1)S(1)} %get-tuple-element.23, f32[8,512]{1,0:T(8,128)S(1)} %get-tuple-element.25, f32[8,512]{1,0:T(8,128)S(1)} %get-tuple-element.26, f32[6]{0:T(128)S(1)} %iota_convert_fusion.1), kind=kOutput, calls=%fused_computation.10 | convolution fusion | flops 12632064 | bytes 1131008 | tf_op jit(solution)/shard_map/while/body/eval_jaxpr/vmap(ik,ic->kc)/dot_general | solution.py:47
  28.3 0.3 fusion.9
  28.7 4.1 %slice_convert_fusion = f32[8,512,256]{2,1,0:T(8,128)} fusion(bf16[8,512,512]{2,1,0:T(8,128)(2,1)} %get-tuple-element.24), kind=kLoop, calls=%fused_computation.12 | loop fusion | flops 1048576 | bytes 6291456 | tf_op jit(solution)/shard_map/while/body/eval_jaxpr/vmap()/convert_element_type | solution.py:63
  32.8 3.8 %broadcast_multiply_fusion = bf16[8,2,512,512]{3,2,1,0:T(8,128)(2,1)} fusion(bf16[8,2,512]{2,1,0:T(2,128)(2,1)S(1)} %convert_bitcast_fusion, bf16[8,512,512]{2,1,0:T(8,128)(2,1)S(1)} %copy-done), kind=kLoop, calls=%fused_computation.7 | loop fusion | flops 4194304 | bytes 12599296 | tf_op jit(solution)/shard_map/while/body/eval_jaxpr/vmap()/mul | solution.py:57
  36.7 5.9 %fusion.5 = f32[8,1024,256]{2,1,0:T(8,128)S(1)} fusion(bf16[8,1024,512]{2,1,0:T(8,128)(2,1)} %bitcast.42, pred[8,512,512]{2,1,0:T(32,128)(4,1)S(1)} %get-tuple-element.23), kind=kOutput, calls=%fused_computation.8 | convolution fusion | flops 2147483648 | bytes 17825792 | tf_op jit(solution)/shard_map/while/body/eval_jaxpr/vmap()/dot_general | solution.py:60
  42.6 4.3 %fusion = f32[8,2,2,256]{3,1,2,0:T(2,128)S(1)} fusion(f32[8,2,512,256]{3,2,1,0:T(8,128)S(1)} %bitcast.41, f32[8,512,256]{2,1,0:T(8,128)S(1)} %copy-done.1, f32[1,8,512]{2,0,1:T(1,128)S(1)} %get-tuple-element.14, f32[1,8,512]{2,0,1:T(1,128)S(1)} %get-tuple-element.13), kind=kOutput, calls=%fused_computation.2 | convolution fusion | flops 52436992 | bytes 12648448 | tf_op jit(solution)/shard_map/while/body/eval_jaxpr/vmap(ai,bik->abk)/dot_general | solution.py:64
  47.0 0.2 convolution_bitcast_fusion
  47.4 2.4 %collective-permute-start.1 = (f32[44,128]{1,0:T(8,128)S(1)}, f32[44,128]{1,0:T(8,128)S(1)}, u32[]{:S(2)}, u32[]{:S(2)}) collective-permute-start(f32[44,128]{1,0:T(8,128)S(1)} %pad_maximum_fusion.2), channel_id=1, source_target_pairs={{0,8},{8,0},{16,24},{24,16},{1,9},{9,1},{17,25},{25,17},{2,10},{10... | collective-permute-start | bytes 67592 | tf_op jit(solution)/shard_map/ppermute | solution.py:23
  49.8 1.8 %collective-permute-done.1 = f32[44,128]{1,0:T(8,128)S(1)} collective-permute-done((f32[44,128]{1,0:T(8,128)S(1)}, f32[44,128]{1,0:T(8,128)S(1)}, u32[]{:S(2)}, u32[]{:S(2)}) %collective-permute-start.1) | collective-permute-done | bytes 22560 | tf_op jit(solution)/shard_map/ppermute | solution.py:23
  51.6 3.1 %collective-permute-start.2 = (f32[44,128]{1,0:T(8,128)S(1)}, f32[44,128]{1,0:T(8,128)S(1)}, u32[]{:S(2)}, u32[]{:S(2)}) collective-permute-start(f32[44,128]{1,0:T(8,128)S(1)} %fusion.26), channel_id=1, source_target_pairs={{0,16},{8,24},{16,0},{24,8},{1,17},{9,25},{17,1},{25,9},{2,18},{10... | collective-permute-start | bytes 67592 | tf_op jit(solution)/shard_map/ppermute | solution.py:23
  54.7 1.8 %collective-permute-done.2 = f32[44,128]{1,0:T(8,128)S(1)} collective-permute-done((f32[44,128]{1,0:T(8,128)S(1)}, f32[44,128]{1,0:T(8,128)S(1)}, u32[]{:S(2)}, u32[]{:S(2)}) %collective-permute-start.2) | collective-permute-done | bytes 22560 | tf_op jit(solution)/shard_map/ppermute | solution.py:23
  56.5 0.6 %slice.62 = f32[8,128]{1,0:T(8,128)} slice(f32[44,128]{1,0:T(8,128)S(1)} %add.9), slice={[36:44], [0:128]} | slice | bytes 8192 | tf_op jit(solution)/shard_map/slice | solution.py:97
  57.1 0.6 %slice.61 = f32[36,128]{1,0:T(8,128)} slice(f32[44,128]{1,0:T(8,128)S(1)} %add.9), slice={[0:36], [0:128]} | slice | bytes 36864 | tf_op jit(solution)/shard_map/slice | solution.py:97
  (33 shorter events, 0.8 us)
Async XLA Ops:
  6.4 10.0 %all-to-all-start = ((f32[8,1,1024]{2,1,0:T(1,128)}), f32[8,1,1024]{2,1,0:T(1,128)S(1)}, u32[]{:S(2)}, u32[]{:S(2)}) async-start(f32[8,1,1024]{2,1,0:T(1,128)} %reshape.186), calls=%async_computation | async-start | bytes 65536 | tf_op jit(solution)/shard_map/all_to_all | solution.py:87
  18.0 5.1 %collective-permute-start = (f32[8,4,256]{2,1,0:T(4,128)S(1)}, f32[8,4,256]{2,1,0:T(4,128)S(1)}, u32[]{:S(2)}, u32[]{:S(2)}) collective-permute-start(f32[8,4,256]{2,1,0:T(4,128)S(1)} %squeeze.22), channel_id=1, source_target_pairs={{0,8},{8,16},{16,24},{1,9},{9,17},{17,25},{2,10},{10,18},{18,26},{... | collective-permute-start | bytes 98312 | tf_op jit(solution)/shard_map/ppermute | solution.py:15
  28.7 4.1 %copy-start = (bf16[8,512,512]{2,1,0:T(8,128)(2,1)S(1)}, bf16[8,512,512]{2,1,0:T(8,128)(2,1)}, u32[]{:S(2)}) copy-start(bf16[8,512,512]{2,1,0:T(8,128)(2,1)} %get-tuple-element.24) | copy-start | bytes 12582916
  36.7 5.9 %copy-start.1 = (f32[8,512,256]{2,1,0:T(8,128)S(1)}, f32[8,512,256]{2,1,0:T(8,128)}, u32[]{:S(2)}) copy-start(f32[8,512,256]{2,1,0:T(8,128)} %slice_convert_fusion) | copy-start | bytes 12582916
  47.4 4.2 %collective-permute-start.1 = (f32[44,128]{1,0:T(8,128)S(1)}, f32[44,128]{1,0:T(8,128)S(1)}, u32[]{:S(2)}, u32[]{:S(2)}) collective-permute-start(f32[44,128]{1,0:T(8,128)S(1)} %pad_maximum_fusion.2), channel_id=1, source_target_pairs={{0,8},{8,0},{16,24},{24,16},{1,9},{9,1},{17,25},{25,17},{2,10},{10... | collective-permute-start | bytes 67592 | tf_op jit(solution)/shard_map/ppermute | solution.py:23
  51.6 4.9 %collective-permute-start.2 = (f32[44,128]{1,0:T(8,128)S(1)}, f32[44,128]{1,0:T(8,128)S(1)}, u32[]{:S(2)}, u32[]{:S(2)}) collective-permute-start(f32[44,128]{1,0:T(8,128)S(1)} %fusion.26), channel_id=1, source_target_pairs={{0,16},{8,24},{16,0},{24,8},{1,17},{9,25},{17,1},{25,9},{2,18},{10... | collective-permute-start | bytes 67592 | tf_op jit(solution)/shard_map/ppermute | solution.py:23

commit v2 on v1

--- a/solution.py
+++ b/solution.py
@@ -3,6 +3,7 @@
 import jax
 import jax.numpy as jnp
 from jax import lax
+from jax.experimental import pallas as pl
 from jax.sharding import PartitionSpec as P
 
 DELTA = 3600
@@ -68,6 +69,76 @@
     return (pairs, triples)
 
 
+def motif_kernel(r_ref, c_ref, pair_ref, trip_ref):
+    n = r_ref.shape[-1]
+    blk = n // 2
+    st_r, lo_r, ki_r, wt_r = (r_ref[0:1, :], r_ref[1:2, :], r_ref[2:3, :], r_ref[3:4, :])
+    st_c, lo_c = (c_ref[:, 0:1], c_ref[:, 1:2])
+    gap = st_r - st_c
+    link = jnp.where((lo_c == lo_r) & (gap > 0.0) & (gap <= DELTA), 1.0, 0.0)
+    link_own = link[:, blk:]
+    link_own16 = link_own.astype(jnp.bfloat16)
+    row = lax.broadcasted_iota(jnp.int32, (8, n), 0).astype(jnp.float32)
+    classes_t = jnp.where(ki_r == row, wt_r, 0.0)
+    earlier_t = jnp.dot(
+        classes_t.astype(jnp.bfloat16), link_own16, preferred_element_type=jnp.float32
+    )
+    lo_o, ki_o, wt_o = (c_ref[blk:, 1:2], c_ref[blk:, 2:3], c_ref[blk:, 3:4])
+    lane = lax.broadcasted_iota(jnp.int32, (blk, 128), 1)
+    lane_acc = (lane % ACC_BLK).astype(jnp.float32)
+    lane_grp = (lane // ACC_BLK).astype(jnp.float32)
+    later = jnp.where((lo_o == lane_acc) & (ki_o == lane_grp), wt_o, 0.0)
+    pair_ref[...] = jnp.dot(
+        earlier_t, later, precision=lax.Precision.HIGHEST, preferred_element_type=jnp.float32
+    )
+    dirs = jnp.where(
+        row == 0.0, jnp.where(ki_r < 2.5, wt_r, 0.0), jnp.where(row == 1.0, jnp.where(ki_r > 2.5, wt_r, 0.0), 0.0)
+    )
+    wt_in = jnp.where(ki_o < 2.5, wt_o, 0.0)
+    wt_out = jnp.where(ki_o > 2.5, wt_o, 0.0)
+    last = jnp.where(
+        lo_o == lane_acc,
+        jnp.where(lane_grp == 0.0, wt_in, jnp.where(lane_grp == 1.0, wt_out, 0.0)),
+        0.0,
+    )
+    for b in range(2):
+        weighted = (link * dirs[b : b + 1, :]).astype(jnp.bfloat16)
+        middle = jnp.dot(weighted, link_own16, preferred_element_type=jnp.float32)
+        closed = middle * link_own
+        ends = jnp.dot(dirs, closed, precision=lax.Precision.HIGHEST, preferred_element_type=jnp.float32)
+        trip_ref[b] = jnp.dot(
+            ends, last, precision=lax.Precision.HIGHEST, preferred_element_type=jnp.float32
+        )
+
+
+def count_blocks(own_events, prior_events):
+    nb, nf, width = own_events.shape
+    fields = jnp.concatenate([prior_events, own_events], axis=2)
+    rows = jnp.concatenate([fields, jnp.zeros((nb, 8 - nf, 2 * width), fields.dtype)], axis=1)
+    cols = fields.transpose(0, 2, 1)
+    pair_out, trip_out = pl.pallas_call(
+        motif_kernel,
+        grid=(nb,),
+        in_specs=[
+            pl.BlockSpec((None, 8, 2 * width), lambda i: (i, 0, 0)),
+            pl.BlockSpec((None, 2 * width, nf), lambda i: (i, 0, 0)),
+        ],
+        out_specs=[
+            pl.BlockSpec((None, 8, 128), lambda i: (i, 0, 0)),
+            pl.BlockSpec((None, 2, 8, 128), lambda i: (i, 0, 0, 0)),
+        ],
+        out_shape=[
+            jax.ShapeDtypeStruct((nb, 8, 128), jnp.float32),
+            jax.ShapeDtypeStruct((nb, 2, 8, 128), jnp.float32),
+        ],
+    )(rows, cols)
+    pairs = pair_out[:, :6, : 6 * ACC_BLK].reshape(nb, 6, 6, ACC_BLK)
+    pairs = pairs.transpose(1, 2, 0, 3).reshape(36, nb * ACC_BLK)
+    triples = trip_out[:, :, :2, : 2 * ACC_BLK].reshape(nb, 2, 2, 2, ACC_BLK)
+    triples = triples.transpose(2, 1, 3, 0, 4).reshape(8, nb * ACC_BLK)
+    return (pairs, triples)
+
+
 def per_device(stamps, account, kind, weight, used):
     owners = lax.axis_size("dev")
     blocks = used.shape[1] // owners
@@ -86,13 +157,7 @@
     )
     own_events = lax.all_to_all(stacked, "dev", split_axis=0, concat_axis=3, tiled=True)[0]
     prior_events = passed_along(own_events, "grp", 1)
-    width = own_events.shape[2]
-    batch = math.gcd(blocks, 16)
-    own_b = own_events.reshape(blocks // batch, batch, 4, width)
-    prior_b = prior_events.reshape(blocks // batch, batch, 4, width)
-    pairs, triples = lax.map(lambda xs: jax.vmap(count_block)(xs[0], xs[1]), (own_b, prior_b))
-    pairs = pairs.reshape(blocks, 36, ACC_BLK).transpose(1, 0, 2).reshape(36, blocks * ACC_BLK)
-    triples = triples.reshape(blocks, 8, ACC_BLK).transpose(1, 0, 2).reshape(8, blocks * ACC_BLK)
+    pairs, triples = count_blocks(own_events, prior_events)
     both = summed_over(jnp.concatenate([pairs, triples], axis=0), "grp")
     return (both[:36], both[36:])
 

time: 58.1 us -> 58.8 us (1.012)
  Pallas kernels: 0 us -> 20.9 us
  other arithmetic: 16.5 us -> 4.25 us
  matrix products: 11.6 us -> 0 us
  blocking collectives: 0 us -> 9.84 us
  starting transfers between devices: 14.2 us -> 8.98 us
  waiting for transfers between devices: 10 us -> 5.19 us
  local copies, waits for them, and re-layouts: 4.6 us -> 8.42 us
    pallas_call x0 -> x1, Pallas kernels: none -> 20.9 us  [count_blocks(): pl.pallas_call(motif_kernel, grid=(nb,), in_specs=[pl.BlockSpec((None, 8,...]
    dot_general x5 -> x0, matrix products: 11.6 us -> none  [the longest x1 5.9 us: count_block(): jnp.dot(weighted, link_own, preferred_element_type=jnp.float32)]
    all_to_all x0 -> x1, blocking collectives: none -> 9.84 us  [per_device(): lax.all_to_all(stacked, 'dev', split_axis=0, concat_axis=3, tiled=True)[0]]
    all_to_all x1 -> x0, starting transfers between devices: 5.2 us -> none  [per_device(): lax.all_to_all(stacked, 'dev', split_axis=0, concat_axis=3, tiled=True)[0]]
    all_to_all x1 -> x0, waiting for transfers between devices: 4.84 us -> none  [per_device(): lax.all_to_all(stacked, 'dev', split_axis=0, concat_axis=3, tiled=True)[0]]
    convert_element_type x3 -> x0, other arithmetic: 4.1 us -> none  [the longest x1 4.09 us: count_block(): closed = middle * link_own.astype(jnp.float32)[None]]
    and x1 -> x0, other arithmetic: 4.08 us -> none  [count_block(): linked = (local[:, None] == local[None, :]) & (gap > 0.0) & (gap <= DELTA)]
    mul x4 -> x0, other arithmetic: 3.98 us -> none  [the longest x1 3.85 us: count_block(): link_all[None, :, :] * dirs.astype(jnp.bfloat16)[:, None, :]]
  transfers between devices with their start and end apart: 4 -> 3, of which waited for: 4 -> 3; matrix products, arithmetic and copies ran while one was open for 0% -> 0% of each run, Pallas kernels for 0% -> 0%
where the time goes in v2:
time: 58.8 us; the launch traced here: 58.3 us
  Pallas kernels  20.9 us (36%)
  blocking collectives  9.84 us (17%)
  starting transfers between devices  8.98 us (15%)
  local copies, waits for them, and re-layouts  8.42 us (14%)
  waiting for transfers between devices  5.19 us (9%)
  other arithmetic  4.25 us (7%)
  between operations  0.73 us (1%)
    pallas_call x1, Pallas kernels, count_blocks(): pl.pallas_call(motif_kernel, grid=(nb,), in_specs=[pl.BlockSpec((None, 8,...  20.9 us
    all_to_all x1, blocking collectives, per_device(): lax.all_to_all(stacked, 'dev', split_axis=0, concat_axis=3, tiled=True)[0]  9.84 us
    ppermute x2, starting transfers between devices, summed_over(): block = block + lax.ppermute(block, axis, [(i, i ^ step) for i in range(n)])  5.5 us
    ppermute x2, waiting for transfers between devices, summed_over(): block = block + lax.ppermute(block, axis, [(i, i ^ step) for i in range(n)])  3.61 us
    ppermute x1, starting transfers between devices, passed_along(): return lax.ppermute(block, axis, route)  3.48 us
    concatenate x3, local copies, waits for them, and re-layouts, count_blocks(): fields = jnp.concatenate([prior_events, own_events], axis=2)  2.05 us
    ppermute x1, waiting for transfers between devices, passed_along(): return lax.ppermute(block, axis, route)  1.58 us
    unnamed x2, other arithmetic  1.33 us
  transfers between devices with their start and end apart: 3, of which 3 were waited for; matrix products, arithmetic and copies ran while one was open for 0% of the time, Pallas kernels for 0%

profile of v2, /device:TPU:0, one launch (start us, length us, event | category | flops | bytes accessed | tf_op | source)
XLA Modules:
  0.0 58.3 jit_solution(18388421818520217491)
XLA Ops:
  0.6 0.5 broadcast.20
  1.1 1.3 %reduce.3 = s32[64]{0:T(128)S(1)} reduce(s32[1,64]{1,0:T(1,128)} %param.9, s32[]{:T(128)} %broadcast.20), dimensions={0}, to_apply=%param.9.reduce_sub_computation.3 | reduce | bytes 516 | tf_op args[4]
  2.5 0.1 gt.22
  2.5 0.7 %convert_element_type.52 = f32[2048]{0:T(1024)S(1)} convert(s32[2048]{0:T(1024)} %param.5) | non-fusion elementwise | flops 2048 | bytes 16384 | tf_op jit(solution)/shard_map/convert_element_type | solution.py:151
  3.2 0.7 %convert_element_type.54 = f32[2048]{0:T(1024)S(1)} convert(s32[2048]{0:T(1024)} %param.6) | non-fusion elementwise | flops 2048 | bytes 16384 | tf_op jit(solution)/shard_map/convert_element_type | solution.py:152
  3.9 0.7 %convert_element_type.56 = f32[2048]{0:T(1024)S(1)} convert(s32[2048]{0:T(1024)} %param.7) | non-fusion elementwise | flops 2048 | bytes 16384 | tf_op jit(solution)/shard_map/convert_element_type | solution.py:153
  4.9 0.8 %reshape.81 = f32[8,8,1,32]{3,1,0,2:T(8,128)S(1)} reshape(bf16[2048]{0:T(1024)(128)(2,1)} %param.8) | data formatting | bytes 12288 | tf_op jit(solution)/shard_map/convert_element_type | solution.py:148
  5.6 0.1 fusion
  5.7 0.1 reshape.91
  5.8 9.8 %all_to_all.15 = f32[8,1,1024]{2,1,0:T(1,128)S(1)} all-to-all(f32[8,1,1024]{2,1,0:T(1,128)S(1)} %reshape.91), channel_id=1, replica_groups=mesh['grp'=4,'dev'=8] {'dev'}, dimensions={0} | all-to-all | bytes 65536 | tf_op jit(solution)/shard_map/all_to_all | solution.py:158
  15.7 0.5 broadcast.21
  16.2 0.7 %reduce.4 = f32[8,1024]{1,0:T(8,128)S(1)} reduce(f32[8,1,1024]{2,1,0:T(1,128)S(1)} %all_to_all.15, f32[]{:T(128)} %broadcast.21), dimensions={1}, to_apply=%all_to_all.11.reduce_sub_computation | reduce | bytes 65540 | tf_op jit(solution)/shard_map/all_to_all | solution.py:158
  16.9 0.1 reshape.92
  17.0 0.1 copy.27
  17.1 0.1 squeeze.3
  17.2 3.5 %collective-permute-start = (f32[8,4,256]{2,0,1:T(8,128)S(1)}, f32[8,4,256]{2,0,1:T(8,128)S(1)}, u32[]{:S(2)}, u32[]{:S(2)}) collective-permute-start(f32[8,4,256]{2,0,1:T(8,128)S(1)} %squeeze.3), channel_id=1, source_target_pairs={{0,8},{8,16},{16,24},{1,9},{9,17},{17,25},{2,10},{10,18},{18,26},{... | collective-permute-start | bytes 98312 | tf_op jit(solution)/shard_map/ppermute | solution.py:16
  20.7 1.6 %collective-permute-done = f32[8,4,256]{2,0,1:T(8,128)S(1)} collective-permute-done((f32[8,4,256]{2,0,1:T(8,128)S(1)}, f32[8,4,256]{2,0,1:T(8,128)S(1)}, u32[]{:S(2)}, u32[]{:S(2)}) %collective-permute-start) | collective-permute-done | bytes 32800 | tf_op jit(solution)/shard_map/ppermute | solution.py:16
  22.3 2.0 %copy.29 = f32[8,4,512]{1,2,0:T(8,128)} copy(f32[8,4,512]{2,0,1:T(8,128)S(1)} %constant_dynamic-update-slice_fusion) | data formatting | bytes 131072 | tf_op jit(solution)/shard_map/concatenate | solution.py:116
  24.3 0.7 %concatenate.10.r_ref = f32[8,8,512]{2,1,0:T(8,128)} pad(f32[8,4,512]{2,1,0:T(4,128)S(1)} %copy.28, f32[]{:T(128)} %constant.1.clone.1), padding=0_0x0_4x0_0 | pad | bytes 196612 | tf_op jit(solution)/shard_map/concatenate | solution.py:117
  25.0 20.9 %shard_map.68 = (f32[8,8,128]{2,1,0:T(8,128)}, f32[8,2,8,128]{3,2,1,0:T(8,128)}) custom-call(f32[8,8,512]{2,1,0:T(8,128)} %concatenate.10.r_ref, f32[8,512,4]{2,1,0:T(8,128)} %bitcast.22), custom_call_target="tpu_custom_call" | custom-call | tf_op jit(solution)/shard_map/pallas_call | solution.py:119
  45.9 0.8 %copy.30 = f32[8,6,96]{2,0,1:T(8,128)S(1)} copy(f32[8,6,96]{2,1,0:T(8,128)} %bitcast.25) | data formatting | bytes 36864 | tf_op jit(solution)/shard_map/slice | solution.py:135
  46.7 0.8 %slice.13 = f32[8,2,2,32]{3,2,1,0:T(2,128)S(1)} slice(f32[8,2,8,128]{3,2,1,0:T(8,128)} %get-tuple-element.5), slice={[0:8], [0:2], [0:2], [0:32]} | slice | bytes 8192 | tf_op jit(solution)/shard_map/slice | solution.py:137
  47.5 0.1 reshape.79
  47.6 0.1 reshape.80
  47.7 0.1 reshape.77
  47.9 0.1 reshape.78
  48.0 2.4 %collective-permute-start.1 = (f32[44,128]{1,0:T(8,128)S(1)}, f32[44,128]{1,0:T(8,128)S(1)}, u32[]{:S(2)}, u32[]{:S(2)}) collective-permute-start(f32[44,128]{1,0:T(8,128)S(1)} %pad_maximum_fusion.1), channel_id=1, source_target_pairs={{0,8},{8,0},{16,24},{24,16},{1,9},{9,1},{17,25},{25,17},{2,10},{10... | collective-permute-start | bytes 67592 | tf_op jit(solution)/shard_map/ppermute | solution.py:24
  50.4 1.8 %collective-permute-done.1 = f32[44,128]{1,0:T(8,128)S(1)} collective-permute-done((f32[44,128]{1,0:T(8,128)S(1)}, f32[44,128]{1,0:T(8,128)S(1)}, u32[]{:S(2)}, u32[]{:S(2)}) %collective-permute-start.1) | collective-permute-done | bytes 22560 | tf_op jit(solution)/shard_map/ppermute | solution.py:24
  52.2 3.1 %collective-permute-start.2 = (f32[44,128]{1,0:T(8,128)S(1)}, f32[44,128]{1,0:T(8,128)S(1)}, u32[]{:S(2)}, u32[]{:S(2)}) collective-permute-start(f32[44,128]{1,0:T(8,128)S(1)} %fusion.1), channel_id=1, source_target_pairs={{0,16},{8,24},{16,0},{24,8},{1,17},{9,25},{17,1},{25,9},{2,18},{10... | collective-permute-start | bytes 67592 | tf_op jit(solution)/shard_map/ppermute | solution.py:24
  55.3 1.8 %collective-permute-done.2 = f32[44,128]{1,0:T(8,128)S(1)} collective-permute-done((f32[44,128]{1,0:T(8,128)S(1)}, f32[44,128]{1,0:T(8,128)S(1)}, u32[]{:S(2)}, u32[]{:S(2)}) %collective-permute-start.2) | collective-permute-done | bytes 22560 | tf_op jit(solution)/shard_map/ppermute | solution.py:24
  57.1 0.6 %slice.17 = f32[8,128]{1,0:T(8,128)} slice(f32[44,128]{1,0:T(8,128)S(1)} %add.9), slice={[36:44], [0:128]} | slice | bytes 8192 | tf_op jit(solution)/shard_map/slice | solution.py:162
  57.7 0.6 %slice.16 = f32[36,128]{1,0:T(8,128)} slice(f32[44,128]{1,0:T(8,128)S(1)} %add.9), slice={[0:36], [0:128]} | slice | bytes 36864 | tf_op jit(solution)/shard_map/slice | solution.py:162
  (13 shorter events, 0.3 us)
Async XLA Ops:
  17.2 5.1 %collective-permute-start = (f32[8,4,256]{2,0,1:T(8,128)S(1)}, f32[8,4,256]{2,0,1:T(8,128)S(1)}, u32[]{:S(2)}, u32[]{:S(2)}) collective-permute-start(f32[8,4,256]{2,0,1:T(8,128)S(1)} %squeeze.3), channel_id=1, source_target_pairs={{0,8},{8,16},{16,24},{1,9},{9,17},{17,25},{2,10},{10,18},{18,26},{... | collective-permute-start | bytes 98312 | tf_op jit(solution)/shard_map/ppermute | solution.py:16
  48.0 4.2 %collective-permute-start.1 = (f32[44,128]{1,0:T(8,128)S(1)}, f32[44,128]{1,0:T(8,128)S(1)}, u32[]{:S(2)}, u32[]{:S(2)}) collective-permute-start(f32[44,128]{1,0:T(8,128)S(1)} %pad_maximum_fusion.1), channel_id=1, source_target_pairs={{0,8},{8,0},{16,24},{24,16},{1,9},{9,1},{17,25},{25,17},{2,10},{10... | collective-permute-start | bytes 67592 | tf_op jit(solution)/shard_map/ppermute | solution.py:24
  52.2 4.9 %collective-permute-start.2 = (f32[44,128]{1,0:T(8,128)S(1)}, f32[44,128]{1,0:T(8,128)S(1)}, u32[]{:S(2)}, u32[]{:S(2)}) collective-permute-start(f32[44,128]{1,0:T(8,128)S(1)} %fusion.1), channel_id=1, source_target_pairs={{0,16},{8,24},{16,0},{24,8},{1,17},{9,25},{17,1},{25,9},{2,18},{10... | collective-permute-start | bytes 67592 | tf_op jit(solution)/shard_map/ppermute | solution.py:24

commit v3 on v2

--- a/solution.py
+++ b/solution.py
@@ -72,12 +72,12 @@
 def motif_kernel(r_ref, c_ref, pair_ref, trip_ref):
     n = r_ref.shape[-1]
     blk = n // 2
-    st_r, lo_r, ki_r, wt_r = (r_ref[0:1, :], r_ref[1:2, :], r_ref[2:3, :], r_ref[3:4, :])
-    st_c, lo_c = (c_ref[:, 0:1], c_ref[:, 1:2])
-    gap = st_r - st_c
-    link = jnp.where((lo_c == lo_r) & (gap > 0.0) & (gap <= DELTA), 1.0, 0.0)
-    link_own = link[:, blk:]
-    link_own16 = link_own.astype(jnp.bfloat16)
+    key_r, ki_r, wt_r = (r_ref[4:5, :], r_ref[2:3, :], r_ref[3:4, :])
+    gap = key_r - c_ref[:, 4:5]
+    linked = (gap > 0.0) & (gap <= DELTA)
+    link16 = jnp.where(linked, 1.0, 0.0).astype(jnp.bfloat16)
+    linked_own = linked[:, blk:]
+    link_own16 = link16[:, blk:]
     row = lax.broadcasted_iota(jnp.int32, (8, n), 0).astype(jnp.float32)
     classes_t = jnp.where(ki_r == row, wt_r, 0.0)
     earlier_t = jnp.dot(
@@ -94,6 +94,15 @@
     dirs = jnp.where(
         row == 0.0, jnp.where(ki_r < 2.5, wt_r, 0.0), jnp.where(row == 1.0, jnp.where(ki_r > 2.5, wt_r, 0.0), 0.0)
     )
+    ki_c, wt_c = (c_ref[:, 2:3], c_ref[:, 3:4])
+    d_in = jnp.where(ki_c < 2.5, wt_c, 0.0)
+    d_out = jnp.where(ki_c > 2.5, wt_c, 0.0)
+    scaled = jnp.concatenate(
+        [jnp.where(linked_own, d_in, 0.0), jnp.where(linked_own, d_out, 0.0)], axis=1
+    ).astype(jnp.bfloat16)
+    middle = jnp.dot(link16, scaled, preferred_element_type=jnp.float32)
+    closed = jnp.where(jnp.concatenate([linked_own, linked_own], axis=1), middle, 0.0)
+    ends = jnp.dot(dirs, closed, precision=lax.Precision.HIGH, preferred_element_type=jnp.float32)
     wt_in = jnp.where(ki_o < 2.5, wt_o, 0.0)
     wt_out = jnp.where(ki_o > 2.5, wt_o, 0.0)
     last = jnp.where(
@@ -102,26 +111,26 @@
         0.0,
     )
     for b in range(2):
-        weighted = (link * dirs[b : b + 1, :]).astype(jnp.bfloat16)
-        middle = jnp.dot(weighted, link_own16, preferred_element_type=jnp.float32)
-        closed = middle * link_own
-        ends = jnp.dot(dirs, closed, precision=lax.Precision.HIGHEST, preferred_element_type=jnp.float32)
         trip_ref[b] = jnp.dot(
-            ends, last, precision=lax.Precision.HIGHEST, preferred_element_type=jnp.float32
+            ends[:, b * blk : (b + 1) * blk],
+            last,
+            precision=lax.Precision.HIGHEST,
+            preferred_element_type=jnp.float32,
         )
 
 
 def count_blocks(own_events, prior_events):
     nb, nf, width = own_events.shape
     fields = jnp.concatenate([prior_events, own_events], axis=2)
-    rows = jnp.concatenate([fields, jnp.zeros((nb, 8 - nf, 2 * width), fields.dtype)], axis=1)
-    cols = fields.transpose(0, 2, 1)
+    key = fields[:, 1:2] * 131072.0 + fields[:, 0:1]
+    rows = jnp.concatenate([fields, key, jnp.zeros((nb, 3, 2 * width), fields.dtype)], axis=1)
+    cols = rows[:, :5].transpose(0, 2, 1)
     pair_out, trip_out = pl.pallas_call(
         motif_kernel,
         grid=(nb,),
         in_specs=[
             pl.BlockSpec((None, 8, 2 * width), lambda i: (i, 0, 0)),
-            pl.BlockSpec((None, 2 * width, nf), lambda i: (i, 0, 0)),
+            pl.BlockSpec((None, 2 * width, 5), lambda i: (i, 0, 0)),
         ],
         out_specs=[
             pl.BlockSpec((None, 8, 128), lambda i: (i, 0, 0)),

time: 58.8 us -> 49.8 us (0.85)
  Pallas kernels: 20.9 us -> 11.7 us
  other arithmetic: 4.25 us -> 4.99 us
    pallas_call x1, Pallas kernels: 20.9 us -> 11.7 us  [count_blocks(): pl.pallas_call(motif_kernel, grid=(nb,), in_specs=[pl.BlockSpec((None, 8,...]
    concatenate x3 -> x2, local copies, waits for them, and re-layouts: 2.05 us -> 0.05 us  [count_blocks(): fields = jnp.concatenate([prior_events, own_events], axis=2)]
    concatenate x1 -> x2, local copies, waits for them, and re-layouts: 0.66 us -> 2.09 us  [count_blocks(): jnp.concatenate([fields, key, jnp.zeros((nb, 3, 2 * width), fields.dtype)...]
    concatenate x0 -> x2, other arithmetic: none -> 0.74 us  [count_blocks(): jnp.concatenate([fields, key, jnp.zeros((nb, 3, 2 * width), fields.dtype)...]
where the time goes in v3:
time: 49.8 us; the launch traced here: 49.3 us
  Pallas kernels  11.7 us (23%)
  blocking collectives  9.84 us (20%)
  starting transfers between devices  8.98 us (18%)
  local copies, waits for them, and re-layouts  7.87 us (16%)
  waiting for transfers between devices  5.1 us (10%)
  other arithmetic  4.99 us (10%)
  between operations  0.76 us (2%)
    pallas_call x1, Pallas kernels, count_blocks(): pl.pallas_call(motif_kernel, grid=(nb,), in_specs=[pl.BlockSpec((None, 8,...  11.7 us
    all_to_all x1, blocking collectives, per_device(): lax.all_to_all(stacked, 'dev', split_axis=0, concat_axis=3, tiled=True)[0]  9.84 us
    ppermute x2, starting transfers between devices, summed_over(): block = block + lax.ppermute(block, axis, [(i, i ^ step) for i in range(n)])  5.49 us
    ppermute x2, waiting for transfers between devices, summed_over(): block = block + lax.ppermute(block, axis, [(i, i ^ step) for i in range(n)])  3.61 us
    ppermute x1, starting transfers between devices, passed_along(): return lax.ppermute(block, axis, route)  3.48 us
    concatenate x2, local copies, waits for them, and re-layouts, count_blocks(): jnp.concatenate([fields, key, jnp.zeros((nb, 3, 2 * width), fields.dtype)...  2.09 us
    ppermute x1, waiting for transfers between devices, passed_along(): return lax.ppermute(block, axis, route)  1.49 us
    unnamed x2, other arithmetic  1.33 us
  transfers between devices with their start and end apart: 3, of which 3 were waited for; matrix products, arithmetic and copies ran while one was open for 0% of the time, Pallas kernels for 0%

profile of v3, /device:TPU:0, one launch (start us, length us, event | category | flops | bytes accessed | tf_op | source)
XLA Modules:
  0.0 49.3 jit_solution(368578080661937686)
XLA Ops:
  0.6 0.5 %broadcast.20 = s32[]{:T(128)} broadcast(s32[]{:T(128)} %constant.27), dimensions={} | broadcast | bytes 8 | tf_op args[4]
  1.1 1.3 %reduce.3 = s32[64]{0:T(128)S(1)} reduce(s32[1,64]{1,0:T(1,128)} %param.9, s32[]{:T(128)} %broadcast.20), dimensions={0}, to_apply=%param.9.reduce_sub_computation.3 | reduce | bytes 516 | tf_op args[4]
  2.5 0.1 gt.22
  2.5 0.7 %convert_element_type.52 = f32[2048]{0:T(1024)S(1)} convert(s32[2048]{0:T(1024)} %param.5) | non-fusion elementwise | flops 2048 | bytes 16384 | tf_op jit(solution)/shard_map/convert_element_type | solution.py:160
  3.2 0.7 %convert_element_type.54 = f32[2048]{0:T(1024)S(1)} convert(s32[2048]{0:T(1024)} %param.6) | non-fusion elementwise | flops 2048 | bytes 16384 | tf_op jit(solution)/shard_map/convert_element_type | solution.py:161
  3.9 0.7 %convert_element_type.56 = f32[2048]{0:T(1024)S(1)} convert(s32[2048]{0:T(1024)} %param.7) | non-fusion elementwise | flops 2048 | bytes 16384 | tf_op jit(solution)/shard_map/convert_element_type | solution.py:162
  4.9 0.8 %reshape.81 = f32[8,8,1,32]{3,1,0,2:T(8,128)S(1)} reshape(bf16[2048]{0:T(1024)(128)(2,1)} %param.8) | data formatting | bytes 12288 | tf_op jit(solution)/shard_map/convert_element_type | solution.py:157
  5.6 0.1 fusion
  5.7 0.1 reshape.91
  5.8 9.8 %all_to_all.15 = f32[8,1,1024]{2,1,0:T(1,128)S(1)} all-to-all(f32[8,1,1024]{2,1,0:T(1,128)S(1)} %reshape.91), channel_id=1, replica_groups=mesh['grp'=4,'dev'=8] {'dev'}, dimensions={0} | all-to-all | bytes 65536 | tf_op jit(solution)/shard_map/all_to_all | solution.py:167
  15.7 0.5 %broadcast.21 = f32[]{:T(128)} broadcast(f32[]{:T(128)} %constant.29), dimensions={} | broadcast | bytes 8 | tf_op jit(solution)/shard_map/all_to_all | solution.py:167
  16.2 0.7 %reduce.4 = f32[8,1024]{1,0:T(8,128)S(1)} reduce(f32[8,1,1024]{2,1,0:T(1,128)S(1)} %all_to_all.15, f32[]{:T(128)} %broadcast.21), dimensions={1}, to_apply=%all_to_all.11.reduce_sub_computation | reduce | bytes 65540 | tf_op jit(solution)/shard_map/all_to_all | solution.py:167
  16.9 0.1 reshape.92
  17.0 0.1 copy.28
  17.1 0.1 squeeze.3
  17.2 3.5 %collective-permute-start = (f32[8,4,256]{2,0,1:T(8,128)S(1)}, f32[8,4,256]{2,0,1:T(8,128)S(1)}, u32[]{:S(2)}, u32[]{:S(2)}) collective-permute-start(f32[8,4,256]{2,0,1:T(8,128)S(1)} %squeeze.3), channel_id=1, source_target_pairs={{0,8},{8,16},{16,24},{1,9},{9,17},{17,25},{2,10},{10,18},{18,26},{... | collective-permute-start | bytes 98312 | tf_op jit(solution)/shard_map/ppermute | solution.py:16
  20.8 1.5 %collective-permute-done = f32[8,4,256]{2,0,1:T(8,128)S(1)} collective-permute-done((f32[8,4,256]{2,0,1:T(8,128)S(1)}, f32[8,4,256]{2,0,1:T(8,128)S(1)}, u32[]{:S(2)}, u32[]{:S(2)}) %collective-permute-start) | collective-permute-done | bytes 32800 | tf_op jit(solution)/shard_map/ppermute | solution.py:16
  22.4 2.0 %copy.31 = f32[8,5,512]{1,2,0:T(8,128)} copy(f32[8,5,512]{2,0,1:T(8,128)S(1)} %pad_maximum_fusion.1) | data formatting | bytes 163840 | tf_op jit(solution)/shard_map/concatenate | solution.py:126
  24.4 0.7 %maximum_maximum_fusion.r_ref = f32[8,8,512]{2,1,0:T(8,128)} fusion(f32[8,1,512]{2,1,0:T(1,128)S(1)} %copy.30, f32[8,4,512]{2,1,0:T(4,128)S(1)} %copy.29, f32[8]{0:T(128)S(1)} %pad.6.clone), kind=kLoop, calls=%fused_computation.1 | loop fusion | flops 65536 | bytes 213024 | tf_op jit(solution)/shard_map/concatenate | solution.py:126
  25.1 11.7 %shard_map.68 = (f32[8,8,128]{2,1,0:T(8,128)}, f32[8,2,8,128]{3,2,1,0:T(8,128)}) custom-call(f32[8,8,512]{2,1,0:T(8,128)} %maximum_maximum_fusion.r_ref, f32[8,512,5]{2,1,0:T(8,128)} %bitcast.22), custom_call_target="tpu_custom_call" | custom-call | tf_op jit(solution)/shard_map/pallas_call | solution.py:128
  36.9 0.8 %copy.32 = f32[8,6,96]{2,0,1:T(8,128)S(1)} copy(f32[8,6,96]{2,1,0:T(8,128)} %bitcast.25) | data formatting | bytes 36864 | tf_op jit(solution)/shard_map/slice | solution.py:144
  37.6 0.8 %slice.23 = f32[8,2,2,32]{3,2,1,0:T(2,128)S(1)} slice(f32[8,2,8,128]{3,2,1,0:T(8,128)} %get-tuple-element.5), slice={[0:8], [0:2], [0:2], [0:32]} | slice | bytes 8192 | tf_op jit(solution)/shard_map/slice | solution.py:146
  38.5 0.1 reshape.79
  38.6 0.1 reshape.80
  38.7 0.1 reshape.77
  38.8 0.1 reshape.78
  38.9 2.4 %collective-permute-start.1 = (f32[44,128]{1,0:T(8,128)S(1)}, f32[44,128]{1,0:T(8,128)S(1)}, u32[]{:S(2)}, u32[]{:S(2)}) collective-permute-start(f32[44,128]{1,0:T(8,128)S(1)} %pad_maximum_fusion.2), channel_id=1, source_target_pairs={{0,8},{8,0},{16,24},{24,16},{1,9},{9,1},{17,25},{25,17},{2,10},{10... | collective-permute-start | bytes 67592 | tf_op jit(solution)/shard_map/ppermute | solution.py:24
  41.3 1.8 %collective-permute-done.1 = f32[44,128]{1,0:T(8,128)S(1)} collective-permute-done((f32[44,128]{1,0:T(8,128)S(1)}, f32[44,128]{1,0:T(8,128)S(1)}, u32[]{:S(2)}, u32[]{:S(2)}) %collective-permute-start.1) | collective-permute-done | bytes 22560 | tf_op jit(solution)/shard_map/ppermute | solution.py:24
  43.2 3.1 %collective-permute-start.2 = (f32[44,128]{1,0:T(8,128)S(1)}, f32[44,128]{1,0:T(8,128)S(1)}, u32[]{:S(2)}, u32[]{:S(2)}) collective-permute-start(f32[44,128]{1,0:T(8,128)S(1)} %fusion.1), channel_id=1, source_target_pairs={{0,16},{8,24},{16,0},{24,8},{1,17},{9,25},{17,1},{25,9},{2,18},{10... | collective-permute-start | bytes 67592 | tf_op jit(solution)/shard_map/ppermute | solution.py:24
  46.3 1.8 %collective-permute-done.2 = f32[44,128]{1,0:T(8,128)S(1)} collective-permute-done((f32[44,128]{1,0:T(8,128)S(1)}, f32[44,128]{1,0:T(8,128)S(1)}, u32[]{:S(2)}, u32[]{:S(2)}) %collective-permute-start.2) | collective-permute-done | bytes 22560 | tf_op jit(solution)/shard_map/ppermute | solution.py:24
  48.1 0.6 %slice.29 = f32[8,128]{1,0:T(8,128)} slice(f32[44,128]{1,0:T(8,128)S(1)} %add.11), slice={[36:44], [0:128]} | slice | bytes 8192 | tf_op jit(solution)/shard_map/slice | solution.py:171
  48.7 0.6 %slice.28 = f32[36,128]{1,0:T(8,128)} slice(f32[44,128]{1,0:T(8,128)S(1)} %add.11), slice={[0:36], [0:128]} | slice | bytes 36864 | tf_op jit(solution)/shard_map/slice | solution.py:171
  (18 shorter events, 0.5 us)
Async XLA Ops:
  17.2 5.1 %collective-permute-start = (f32[8,4,256]{2,0,1:T(8,128)S(1)}, f32[8,4,256]{2,0,1:T(8,128)S(1)}, u32[]{:S(2)}, u32[]{:S(2)}) collective-permute-start(f32[8,4,256]{2,0,1:T(8,128)S(1)} %squeeze.3), channel_id=1, source_target_pairs={{0,8},{8,16},{16,24},{1,9},{9,17},{17,25},{2,10},{10,18},{18,26},{... | collective-permute-start | bytes 98312 | tf_op jit(solution)/shard_map/ppermute | solution.py:16
  38.9 4.2 %collective-permute-start.1 = (f32[44,128]{1,0:T(8,128)S(1)}, f32[44,128]{1,0:T(8,128)S(1)}, u32[]{:S(2)}, u32[]{:S(2)}) collective-permute-start(f32[44,128]{1,0:T(8,128)S(1)} %pad_maximum_fusion.2), channel_id=1, source_target_pairs={{0,8},{8,0},{16,24},{24,16},{1,9},{9,1},{17,25},{25,17},{2,10},{10... | collective-permute-start | bytes 67592 | tf_op jit(solution)/shard_map/ppermute | solution.py:24
  43.2 4.9 %collective-permute-start.2 = (f32[44,128]{1,0:T(8,128)S(1)}, f32[44,128]{1,0:T(8,128)S(1)}, u32[]{:S(2)}, u32[]{:S(2)}) collective-permute-start(f32[44,128]{1,0:T(8,128)S(1)} %fusion.1), channel_id=1, source_target_pairs={{0,16},{8,24},{16,0},{24,8},{1,17},{9,25},{17,1},{25,9},{2,18},{10... | collective-permute-start | bytes 67592 | tf_op jit(solution)/shard_map/ppermute | solution.py:24

commit v4 on v3

--- a/solution.py
+++ b/solution.py
@@ -69,7 +69,8 @@
     return (pairs, triples)
 
 
-def motif_kernel(r_ref, c_ref, pair_ref, trip_ref):
+def motif_kernel(r_ref, pair_ref, trip_ref):
+    c_ref = jnp.transpose(r_ref[...])
     n = r_ref.shape[-1]
     blk = n // 2
     key_r, ki_r, wt_r = (r_ref[4:5, :], r_ref[2:3, :], r_ref[3:4, :])
@@ -124,13 +125,11 @@
     fields = jnp.concatenate([prior_events, own_events], axis=2)
     key = fields[:, 1:2] * 131072.0 + fields[:, 0:1]
     rows = jnp.concatenate([fields, key, jnp.zeros((nb, 3, 2 * width), fields.dtype)], axis=1)
-    cols = rows[:, :5].transpose(0, 2, 1)
     pair_out, trip_out = pl.pallas_call(
         motif_kernel,
         grid=(nb,),
         in_specs=[
             pl.BlockSpec((None, 8, 2 * width), lambda i: (i, 0, 0)),
-            pl.BlockSpec((None, 2 * width, 5), lambda i: (i, 0, 0)),
         ],
         out_specs=[
             pl.BlockSpec((None, 8, 128), lambda i: (i, 0, 0)),
@@ -140,7 +139,7 @@
             jax.ShapeDtypeStruct((nb, 8, 128), jnp.float32),
             jax.ShapeDtypeStruct((nb, 2, 8, 128), jnp.float32),
         ],
-    )(rows, cols)
+    )(rows)
     pairs = pair_out[:, :6, : 6 * ACC_BLK].reshape(nb, 6, 6, ACC_BLK)
     pairs = pairs.transpose(1, 2, 0, 3).reshape(36, nb * ACC_BLK)
     triples = trip_out[:, :, :2, : 2 * ACC_BLK].reshape(nb, 2, 2, 2, ACC_BLK)

time: 49.8 us -> 48 us (0.964)
  other arithmetic: 4.99 us -> 2.9 us
  Pallas kernels: 11.7 us -> 12.8 us
  local copies, waits for them, and re-layouts: 7.87 us -> 7.12 us
    concatenate x2 -> x1, local copies, waits for them, and re-layouts: 2.09 us -> 0.07 us  [count_blocks(): jnp.concatenate([fields, key, jnp.zeros((nb, 3, 2 * width), fields.dtype)...]
    unnamed x4 -> x12, local copies, waits for them, and re-layouts: 0.72 us -> 2.74 us
    pallas_call x1, Pallas kernels: 11.7 us -> 12.8 us  [count_blocks(): pl.pallas_call(motif_kernel, grid=(nb,), in_specs=[pl.BlockSpec((None, 8,...]
    convert_element_type x1, other arithmetic: 0.7 us -> 0.01 us  [per_device(): stamps.reshape(shape3).astype(jnp.float32)]
    convert_element_type x1, other arithmetic: 0.7 us -> 0.01 us  [per_device(): account.reshape(shape3).astype(jnp.float32)]
    convert_element_type x1, other arithmetic: 0.7 us -> 0.01 us  [per_device(): kind.reshape(shape3).astype(jnp.float32)]
    convert_element_type x1, local copies, waits for them, and re-layouts: 0.77 us -> 0.07 us  [per_device(): weight.reshape(shape3).astype(jnp.float32)]
where the time goes in v4:
time: 48 us; the launch traced here: 47.5 us
  Pallas kernels  12.8 us (27%)
  blocking collectives  9.84 us (20%)
  starting transfers between devices  8.98 us (19%)
  local copies, waits for them, and re-layouts  7.12 us (15%)
  waiting for transfers between devices  5.1 us (11%)
  other arithmetic  2.9 us (6%)
  between operations  0.76 us (2%)
    pallas_call x1, Pallas kernels, count_blocks(): pl.pallas_call(motif_kernel, grid=(nb,), in_specs=[pl.BlockSpec((None, 8,...  12.8 us
    all_to_all x1, blocking collectives, per_device(): lax.all_to_all(stacked, 'dev', split_axis=0, concat_axis=3, tiled=True)[0]  9.84 us
    ppermute x2, starting transfers between devices, summed_over(): block = block + lax.ppermute(block, axis, [(i, i ^ step) for i in range(n)])  5.49 us
    ppermute x2, waiting for transfers between devices, summed_over(): block = block + lax.ppermute(block, axis, [(i, i ^ step) for i in range(n)])  3.61 us
    ppermute x1, starting transfers between devices, passed_along(): return lax.ppermute(block, axis, route)  3.48 us
    unnamed x12, local copies, waits for them, and re-layouts  2.74 us
    ppermute x1, waiting for transfers between devices, passed_along(): return lax.ppermute(block, axis, route)  1.49 us
    unnamed x2, other arithmetic  1.33 us
  transfers between devices with their start and end apart: 3, of which 3 were waited for; matrix products, arithmetic and copies ran while one was open for 0% of the time, Pallas kernels for 0%

profile of v4, /device:TPU:0, one launch (start us, length us, event | category | flops | bytes accessed | tf_op | source)
XLA Modules:
  0.0 47.5 jit_solution(12783512252882720287)
XLA Ops:
  0.6 0.5 %broadcast.20 = s32[]{:T(128)} broadcast(s32[]{:T(128)} %constant.25), dimensions={} | broadcast | bytes 8 | tf_op args[4]
  1.2 1.3 %reduce.3 = s32[64]{0:T(128)S(1)} reduce(s32[1,64]{1,0:T(1,128)} %param.9, s32[]{:T(128)} %broadcast.20), dimensions={0}, to_apply=%param.9.reduce_sub_computation.3 | reduce | bytes 516 | tf_op args[4]
  2.5 0.1 gt.22
  2.6 0.7 %copy-done.1 = s32[2048]{0:T(1024)S(1)} copy-done((s32[2048]{0:T(1024)S(1)}, s32[2048]{0:T(1024)}, u32[]{:S(2)}) %copy-start.1) | copy-done | bytes 8216
  3.3 0.7 %copy-done.2 = s32[2048]{0:T(1024)S(1)} copy-done((s32[2048]{0:T(1024)S(1)}, s32[2048]{0:T(1024)}, u32[]{:S(2)}) %copy-start.2) | copy-done | bytes 8216
  4.0 0.1 convert_element_type.57
  4.2 0.6 %copy-done.3 = bf16[2048]{0:T(1024)(128)(2,1)S(1)} copy-done((bf16[2048]{0:T(1024)(128)(2,1)S(1)}, bf16[2048]{0:T(1024)(128)(2,1)}, u32[]{:S(2)}) %copy-start.3) | copy-done | bytes 4120
  4.9 0.1 fusion
  5.0 0.1 reshape.91
  5.1 9.8 %all_to_all.15 = f32[8,1,1024]{2,1,0:T(1,128)S(1)} all-to-all(f32[8,1,1024]{2,1,0:T(1,128)S(1)} %reshape.91), channel_id=1, replica_groups=mesh['grp'=4,'dev'=8] {'dev'}, dimensions={0} | all-to-all | bytes 65536 | tf_op jit(solution)/shard_map/all_to_all | solution.py:166
  14.9 0.5 %broadcast.21 = f32[]{:T(128)} broadcast(f32[]{:T(128)} %constant.27), dimensions={} | broadcast | bytes 8 | tf_op jit(solution)/shard_map/all_to_all | solution.py:166
  15.4 0.7 %reduce.4 = f32[8,1024]{1,0:T(8,128)S(1)} reduce(f32[8,1,1024]{2,1,0:T(1,128)S(1)} %all_to_all.15, f32[]{:T(128)} %broadcast.21), dimensions={1}, to_apply=%all_to_all.11.reduce_sub_computation | reduce | bytes 65540 | tf_op jit(solution)/shard_map/all_to_all | solution.py:166
  16.2 0.1 reshape.92
  16.3 0.1 copy.18
  16.4 0.1 squeeze.3
  16.5 3.5 %collective-permute-start = (f32[8,4,256]{2,1,0:T(4,128)S(1)}, f32[8,4,256]{2,1,0:T(4,128)S(1)}, u32[]{:S(2)}, u32[]{:S(2)}) collective-permute-start(f32[8,4,256]{2,1,0:T(4,128)S(1)} %squeeze.3), channel_id=1, source_target_pairs={{0,8},{8,16},{16,24},{1,9},{9,17},{17,25},{2,10},{10,18},{18,26},{... | collective-permute-start | bytes 98312 | tf_op jit(solution)/shard_map/ppermute | solution.py:16
  20.0 0.1 pad.4.clone
  20.0 1.5 %collective-permute-done = f32[8,4,256]{2,1,0:T(4,128)S(1)} collective-permute-done((f32[8,4,256]{2,1,0:T(4,128)S(1)}, f32[8,4,256]{2,1,0:T(4,128)S(1)}, u32[]{:S(2)}, u32[]{:S(2)}) %collective-permute-start) | collective-permute-done | bytes 32800 | tf_op jit(solution)/shard_map/ppermute | solution.py:16
  21.6 0.7 %maximum_maximum_fusion.r_ref = f32[8,8,512]{2,1,0:T(8,128)} fusion(f32[8,1,512]{2,1,0:T(1,128)S(1)} %slice_add_fusion, f32[8,4,512]{2,1,0:T(4,128)S(1)} %constant_dynamic-update-slice_fusion, f32[8]{0:T(128)S(1)} %pad.4.clone), kind=kLoop, calls=%fused_computation.1 | loop fusion | flops 65536 | bytes 213024 | tf_op jit(solution)/shard_map/concatenate | solution.py:127
  22.3 12.8 %shard_map.68 = (f32[8,8,128]{2,1,0:T(8,128)}, f32[8,2,8,128]{3,2,1,0:T(8,128)}) custom-call(f32[8,8,512]{2,1,0:T(8,128)} %maximum_maximum_fusion.r_ref), custom_call_target="tpu_custom_call" | custom-call | tf_op jit(solution)/shard_map/pallas_call | solution.py:128
  35.1 0.8 %copy.19 = f32[8,6,96]{2,0,1:T(8,128)S(1)} copy(f32[8,6,96]{2,1,0:T(8,128)} %bitcast.21) | data formatting | bytes 36864 | tf_op jit(solution)/shard_map/slice | solution.py:143
  35.8 0.8 %slice.21 = f32[8,2,2,32]{3,2,1,0:T(2,128)S(1)} slice(f32[8,2,8,128]{3,2,1,0:T(8,128)} %get-tuple-element.5), slice={[0:8], [0:2], [0:2], [0:32]} | slice | bytes 8192 | tf_op jit(solution)/shard_map/slice | solution.py:145
  36.7 0.1 reshape.79
  36.8 0.1 reshape.80
  36.9 0.1 reshape.77
  37.0 0.1 reshape.78
  37.1 2.4 %collective-permute-start.1 = (f32[44,128]{1,0:T(8,128)S(1)}, f32[44,128]{1,0:T(8,128)S(1)}, u32[]{:S(2)}, u32[]{:S(2)}) collective-permute-start(f32[44,128]{1,0:T(8,128)S(1)} %pad_maximum_fusion.1), channel_id=1, source_target_pairs={{0,8},{8,0},{16,24},{24,16},{1,9},{9,1},{17,25},{25,17},{2,10},{10... | collective-permute-start | bytes 67592 | tf_op jit(solution)/shard_map/ppermute | solution.py:24
  39.5 1.8 %collective-permute-done.1 = f32[44,128]{1,0:T(8,128)S(1)} collective-permute-done((f32[44,128]{1,0:T(8,128)S(1)}, f32[44,128]{1,0:T(8,128)S(1)}, u32[]{:S(2)}, u32[]{:S(2)}) %collective-permute-start.1) | collective-permute-done | bytes 22560 | tf_op jit(solution)/shard_map/ppermute | solution.py:24
  41.3 3.1 %collective-permute-start.2 = (f32[44,128]{1,0:T(8,128)S(1)}, f32[44,128]{1,0:T(8,128)S(1)}, u32[]{:S(2)}, u32[]{:S(2)}) collective-permute-start(f32[44,128]{1,0:T(8,128)S(1)} %fusion.1), channel_id=1, source_target_pairs={{0,16},{8,24},{16,0},{24,8},{1,17},{9,25},{17,1},{25,9},{2,18},{10... | collective-permute-start | bytes 67592 | tf_op jit(solution)/shard_map/ppermute | solution.py:24
  44.5 1.8 %collective-permute-done.2 = f32[44,128]{1,0:T(8,128)S(1)} collective-permute-done((f32[44,128]{1,0:T(8,128)S(1)}, f32[44,128]{1,0:T(8,128)S(1)}, u32[]{:S(2)}, u32[]{:S(2)}) %collective-permute-start.2) | collective-permute-done | bytes 22560 | tf_op jit(solution)/shard_map/ppermute | solution.py:24
  46.3 0.6 %slice.27 = f32[8,128]{1,0:T(8,128)} slice(f32[44,128]{1,0:T(8,128)S(1)} %add.11), slice={[36:44], [0:128]} | slice | bytes 8192 | tf_op jit(solution)/shard_map/slice | solution.py:170
  46.9 0.6 %slice.26 = f32[36,128]{1,0:T(8,128)} slice(f32[44,128]{1,0:T(8,128)S(1)} %add.11), slice={[0:36], [0:128]} | slice | bytes 36864 | tf_op jit(solution)/shard_map/slice | solution.py:170
  (22 shorter events, 0.4 us)
Async XLA Ops:
  0.6 1.9 %copy-start = (s32[2048]{0:T(1024)S(1)}, s32[2048]{0:T(1024)}, u32[]{:S(2)}) copy-start(s32[2048]{0:T(1024)} %param.5) | copy-start | bytes 24580
  2.6 0.7 %copy-start.1 = (s32[2048]{0:T(1024)S(1)}, s32[2048]{0:T(1024)}, u32[]{:S(2)}) copy-start(s32[2048]{0:T(1024)} %param.6) | copy-start | bytes 24580
  3.3 0.7 %copy-start.2 = (s32[2048]{0:T(1024)S(1)}, s32[2048]{0:T(1024)}, u32[]{:S(2)}) copy-start(s32[2048]{0:T(1024)} %param.7) | copy-start | bytes 24580
  4.1 0.7 %copy-start.3 = (bf16[2048]{0:T(1024)(128)(2,1)S(1)}, bf16[2048]{0:T(1024)(128)(2,1)}, u32[]{:S(2)}) copy-start(bf16[2048]{0:T(1024)(128)(2,1)} %param.8) | copy-start | bytes 12292
  16.5 5.1 %collective-permute-start = (f32[8,4,256]{2,1,0:T(4,128)S(1)}, f32[8,4,256]{2,1,0:T(4,128)S(1)}, u32[]{:S(2)}, u32[]{:S(2)}) collective-permute-start(f32[8,4,256]{2,1,0:T(4,128)S(1)} %squeeze.3), channel_id=1, source_target_pairs={{0,8},{8,16},{16,24},{1,9},{9,17},{17,25},{2,10},{10,18},{18,26},{... | collective-permute-start | bytes 98312 | tf_op jit(solution)/shard_map/ppermute | solution.py:16
  37.1 4.2 %collective-permute-start.1 = (f32[44,128]{1,0:T(8,128)S(1)}, f32[44,128]{1,0:T(8,128)S(1)}, u32[]{:S(2)}, u32[]{:S(2)}) collective-permute-start(f32[44,128]{1,0:T(8,128)S(1)} %pad_maximum_fusion.1), channel_id=1, source_target_pairs={{0,8},{8,0},{16,24},{24,16},{1,9},{9,1},{17,25},{25,17},{2,10},{10... | collective-permute-start | bytes 67592 | tf_op jit(solution)/shard_map/ppermute | solution.py:24
  41.3 4.9 %collective-permute-start.2 = (f32[44,128]{1,0:T(8,128)S(1)}, f32[44,128]{1,0:T(8,128)S(1)}, u32[]{:S(2)}, u32[]{:S(2)}) collective-permute-start(f32[44,128]{1,0:T(8,128)S(1)} %fusion.1), channel_id=1, source_target_pairs={{0,16},{8,24},{16,0},{24,8},{1,17},{9,25},{17,1},{25,9},{2,18},{10... | collective-permute-start | bytes 67592 | tf_op jit(solution)/shard_map/ppermute | solution.py:24

commit v5 on v4

--- a/solution.py
+++ b/solution.py
@@ -166,8 +166,9 @@
     own_events = lax.all_to_all(stacked, "dev", split_axis=0, concat_axis=3, tiled=True)[0]
     prior_events = passed_along(own_events, "grp", 1)
     pairs, triples = count_blocks(own_events, prior_events)
-    both = summed_over(jnp.concatenate([pairs, triples], axis=0), "grp")
-    return (both[:36], both[36:])
+    gap_rows = jnp.zeros((4, pairs.shape[1]), pairs.dtype)
+    both = summed_over(jnp.concatenate([pairs, gap_rows, triples], axis=0), "grp")
+    return (both[:36], both[40:])
 
 
 def solution(mesh):

time: 48 us -> 47.2 us (0.983)
  other arithmetic: 2.9 us -> 2.38 us
    slice x1, local copies, waits for them, and re-layouts: 0.76 us -> 0.01 us  [count_blocks(): pairs = pair_out[:, :6, :6 * ACC_BLK].reshape(nb, 6, 6, ACC_BLK)]
    convert_element_type x1, local copies, waits for them, and re-layouts: 0.07 us -> 0.77 us  [per_device(): weight.reshape(shape3).astype(jnp.float32)]
    unnamed x2, other arithmetic: 1.33 us -> 0.68 us
    unnamed x12 -> x14, local copies, waits for them, and re-layouts: 2.74 us -> 2.65 us
where the time goes in v5:
time: 47.2 us; the launch traced here: 46.7 us
  Pallas kernels  12.8 us (27%)
  blocking collectives  9.84 us (21%)
  starting transfers between devices  8.85 us (19%)
  local copies, waits for them, and re-layouts  7.05 us (15%)
  waiting for transfers between devices  5.03 us (11%)
  other arithmetic  2.38 us (5%)
  between operations  0.77 us (2%)
    pallas_call x1, Pallas kernels, count_blocks(): pl.pallas_call(motif_kernel, grid=(nb,), in_specs=[pl.BlockSpec((None, 8,...  12.8 us
    all_to_all x1, blocking collectives, per_device(): lax.all_to_all(stacked, 'dev', split_axis=0, concat_axis=3, tiled=True)[0]  9.84 us
    ppermute x2, starting transfers between devices, summed_over(): block = block + lax.ppermute(block, axis, [(i, i ^ step) for i in range(n)])  5.37 us
    ppermute x2, waiting for transfers between devices, summed_over(): block = block + lax.ppermute(block, axis, [(i, i ^ step) for i in range(n)])  3.61 us
    ppermute x1, starting transfers between devices, passed_along(): return lax.ppermute(block, axis, route)  3.48 us
    unnamed x14, local copies, waits for them, and re-layouts  2.65 us
    ppermute x1, waiting for transfers between devices, passed_along(): return lax.ppermute(block, axis, route)  1.41 us
    slice x2, local copies, waits for them, and re-layouts, per_device(): return (both[:36], both[40:])  1.2 us
  transfers between devices with their start and end apart: 3, of which 3 were waited for; matrix products, arithmetic and copies ran while one was open for 0% of the time, Pallas kernels for 0%

profile of v5, /device:TPU:0, one launch (start us, length us, event | category | flops | bytes accessed | tf_op | source)
XLA Modules:
  0.0 46.7 jit_solution(1464629482583346207)
XLA Ops:
  0.6 0.8 %reshape.81 = f32[8,8,1,32]{3,1,0,2:T(8,128)S(1)} reshape(bf16[2048]{0:T(1024)(128)(2,1)} %param.8) | data formatting | bytes 12288 | tf_op jit(solution)/shard_map/convert_element_type | solution.py:156
  1.4 0.5 %broadcast.22 = s32[]{:T(128)} broadcast(s32[]{:T(128)} %constant.23), dimensions={} | broadcast | bytes 8 | tf_op args[4]
  1.9 0.7 %reduce.3 = s32[64]{0:T(128)S(1)} reduce(s32[1,64]{1,0:T(1,128)S(1)} %copy-done.4, s32[]{:T(128)} %broadcast.22), dimensions={0}, to_apply=%param.9.reduce_sub_computation.3 | reduce | bytes 516 | tf_op args[4]
  2.6 0.1 gt.22
  2.8 0.6 %copy-done.2 = s32[2048]{0:T(1024)S(1)} copy-done((s32[2048]{0:T(1024)S(1)}, s32[2048]{0:T(1024)}, u32[]{:S(2)}) %copy-start.2) | copy-done | bytes 8216
  3.5 0.6 %copy-done.3 = s32[2048]{0:T(1024)S(1)} copy-done((s32[2048]{0:T(1024)S(1)}, s32[2048]{0:T(1024)}, u32[]{:S(2)}) %copy-start.3) | copy-done | bytes 8216
  4.2 0.1 reshape.91
  4.4 9.8 %all_to_all.15 = f32[8,1,1024]{2,1,0:T(1,128)S(1)} all-to-all(f32[8,1,1024]{2,1,0:T(1,128)S(1)} %reshape.91), channel_id=1, replica_groups=mesh['grp'=4,'dev'=8] {'dev'}, dimensions={0} | all-to-all | bytes 65536 | tf_op jit(solution)/shard_map/all_to_all | solution.py:166
  14.2 0.5 %broadcast.25 = f32[]{:T(128)} broadcast(f32[]{:T(128)} %constant.28), dimensions={} | broadcast | bytes 8 | tf_op jit(solution)/shard_map/all_to_all | solution.py:166
  14.7 0.7 %reduce.4 = f32[8,1024]{1,0:T(8,128)S(1)} reduce(f32[8,1,1024]{2,1,0:T(1,128)S(1)} %all_to_all.15, f32[]{:T(128)} %broadcast.25), dimensions={1}, to_apply=%all_to_all.11.reduce_sub_computation | reduce | bytes 65540 | tf_op jit(solution)/shard_map/all_to_all | solution.py:166
  15.5 0.1 reshape.92
  15.6 0.1 copy.18
  15.6 0.1 squeeze.3
  15.8 3.5 %collective-permute-start = (f32[8,4,256]{2,1,0:T(4,128)S(1)}, f32[8,4,256]{2,1,0:T(4,128)S(1)}, u32[]{:S(2)}, u32[]{:S(2)}) collective-permute-start(f32[8,4,256]{2,1,0:T(4,128)S(1)} %squeeze.3), channel_id=1, source_target_pairs={{0,8},{8,16},{16,24},{1,9},{9,17},{17,25},{2,10},{10,18},{18,26},{... | collective-permute-start | bytes 98312 | tf_op jit(solution)/shard_map/ppermute | solution.py:16
  19.3 0.1 pad.5.clone
  19.3 0.1 pad.1.clone
  19.4 1.4 %collective-permute-done = f32[8,4,256]{2,1,0:T(4,128)S(1)} collective-permute-done((f32[8,4,256]{2,1,0:T(4,128)S(1)}, f32[8,4,256]{2,1,0:T(4,128)S(1)}, u32[]{:S(2)}, u32[]{:S(2)}) %collective-permute-start) | collective-permute-done | bytes 32800 | tf_op jit(solution)/shard_map/ppermute | solution.py:16
  20.9 0.7 %maximum_maximum_fusion.r_ref = f32[8,8,512]{2,1,0:T(8,128)} fusion(f32[8,1,512]{2,1,0:T(1,128)S(1)} %slice_add_fusion, f32[8,4,512]{2,1,0:T(4,128)S(1)} %constant_dynamic-update-slice_fusion, f32[8]{0:T(128)S(1)} %pad.5.clone), kind=kLoop, calls=%fused_computation.1 | loop fusion | flops 65536 | bytes 213024 | tf_op jit(solution)/shard_map/concatenate | solution.py:127
  21.6 12.8 %shard_map.68 = (f32[8,8,128]{2,1,0:T(8,128)}, f32[8,2,8,128]{3,2,1,0:T(8,128)}) custom-call(f32[8,8,512]{2,1,0:T(8,128)} %maximum_maximum_fusion.r_ref), custom_call_target="tpu_custom_call" | custom-call | tf_op jit(solution)/shard_map/pallas_call | solution.py:128
  34.4 0.8 %slice.21 = f32[8,2,2,32]{3,2,1,0:T(2,128)S(1)} slice(f32[8,2,8,128]{3,2,1,0:T(8,128)} %get-tuple-element.5), slice={[0:8], [0:2], [0:2], [0:32]} | slice | bytes 8192 | tf_op jit(solution)/shard_map/slice | solution.py:145
  35.2 0.1 reshape.79
  35.3 0.1 reshape.80
  35.4 0.7 %copy-done = f32[8,8,128]{2,1,0:T(8,128)S(1)} copy-done((f32[8,8,128]{2,1,0:T(8,128)S(1)}, f32[8,8,128]{2,1,0:T(8,128)}, u32[]{:S(2)}) %copy-start) | copy-done | bytes 32792
  36.1 0.1 reshape.77
  36.2 0.1 reshape.78
  36.3 0.1 pad_maximum_fusion.1
  36.4 2.3 %collective-permute-start.1 = (f32[48,128]{1,0:T(8,128)S(1)}, f32[48,128]{1,0:T(8,128)S(1)}, u32[]{:S(2)}, u32[]{:S(2)}) collective-permute-start(f32[48,128]{1,0:T(8,128)S(1)} %pad_maximum_fusion.1), channel_id=1, source_target_pairs={{0,8},{8,0},{16,24},{24,16},{1,9},{9,1},{17,25},{25,17},{2,10},{10... | collective-permute-start | bytes 73736 | tf_op jit(solution)/shard_map/ppermute | solution.py:24
  38.7 1.8 %collective-permute-done.1 = f32[48,128]{1,0:T(8,128)S(1)} collective-permute-done((f32[48,128]{1,0:T(8,128)S(1)}, f32[48,128]{1,0:T(8,128)S(1)}, u32[]{:S(2)}, u32[]{:S(2)}) %collective-permute-start.1) | collective-permute-done | bytes 24608 | tf_op jit(solution)/shard_map/ppermute | solution.py:24
  40.6 3.0 %collective-permute-start.2 = (f32[48,128]{1,0:T(8,128)S(1)}, f32[48,128]{1,0:T(8,128)S(1)}, u32[]{:S(2)}, u32[]{:S(2)}) collective-permute-start(f32[48,128]{1,0:T(8,128)S(1)} %fusion.1), channel_id=1, source_target_pairs={{0,16},{8,24},{16,0},{24,8},{1,17},{9,25},{17,1},{25,9},{2,18},{10... | collective-permute-start | bytes 73736 | tf_op jit(solution)/shard_map/ppermute | solution.py:24
  43.7 1.8 %collective-permute-done.2 = f32[48,128]{1,0:T(8,128)S(1)} collective-permute-done((f32[48,128]{1,0:T(8,128)S(1)}, f32[48,128]{1,0:T(8,128)S(1)}, u32[]{:S(2)}, u32[]{:S(2)}) %collective-permute-start.2) | collective-permute-done | bytes 24608 | tf_op jit(solution)/shard_map/ppermute | solution.py:24
  45.5 0.6 %slice.26 = f32[36,128]{1,0:T(8,128)} slice(f32[48,128]{1,0:T(8,128)S(1)} %add.11), slice={[0:36], [0:128]} | slice | bytes 36864 | tf_op jit(solution)/shard_map/slice | solution.py:171
  46.1 0.6 %slice.27 = f32[8,128]{1,0:T(8,128)} slice(f32[48,128]{1,0:T(8,128)S(1)} %add.11), slice={[40:48], [0:128]} | slice | bytes 8192 | tf_op jit(solution)/shard_map/slice | solution.py:171
  (26 shorter events, 0.5 us)
Async XLA Ops:
  0.6 1.3 %copy-start.4 = (s32[1,64]{1,0:T(1,128)S(1)}, s32[1,64]{1,0:T(1,128)}, u32[]{:S(2)}) copy-start(s32[1,64]{1,0:T(1,128)} %param.9) | copy-start | bytes 772
  1.4 1.3 %copy-start.1 = (s32[2048]{0:T(1024)S(1)}, s32[2048]{0:T(1024)}, u32[]{:S(2)}) copy-start(s32[2048]{0:T(1024)} %param.7) | copy-start | bytes 24580
  2.7 0.7 %copy-start.2 = (s32[2048]{0:T(1024)S(1)}, s32[2048]{0:T(1024)}, u32[]{:S(2)}) copy-start(s32[2048]{0:T(1024)} %param.6) | copy-start | bytes 24580
  3.4 0.7 %copy-start.3 = (s32[2048]{0:T(1024)S(1)}, s32[2048]{0:T(1024)}, u32[]{:S(2)}) copy-start(s32[2048]{0:T(1024)} %param.5) | copy-start | bytes 24580
  15.8 5.1 %collective-permute-start = (f32[8,4,256]{2,1,0:T(4,128)S(1)}, f32[8,4,256]{2,1,0:T(4,128)S(1)}, u32[]{:S(2)}, u32[]{:S(2)}) collective-permute-start(f32[8,4,256]{2,1,0:T(4,128)S(1)} %squeeze.3), channel_id=1, source_target_pairs={{0,8},{8,16},{16,24},{1,9},{9,17},{17,25},{2,10},{10,18},{18,26},{... | collective-permute-start | bytes 98312 | tf_op jit(solution)/shard_map/ppermute | solution.py:16
  35.3 0.8 %copy-start = (f32[8,8,128]{2,1,0:T(8,128)S(1)}, f32[8,8,128]{2,1,0:T(8,128)}, u32[]{:S(2)}) copy-start(f32[8,8,128]{2,1,0:T(8,128)} %get-tuple-element.4) | copy-start | bytes 98308
  36.4 4.1 %collective-permute-start.1 = (f32[48,128]{1,0:T(8,128)S(1)}, f32[48,128]{1,0:T(8,128)S(1)}, u32[]{:S(2)}, u32[]{:S(2)}) collective-permute-start(f32[48,128]{1,0:T(8,128)S(1)} %pad_maximum_fusion.1), channel_id=1, source_target_pairs={{0,8},{8,0},{16,24},{24,16},{1,9},{9,1},{17,25},{25,17},{2,10},{10... | collective-permute-start | bytes 73736 | tf_op jit(solution)/shard_map/ppermute | solution.py:24
  40.6 4.8 %collective-permute-start.2 = (f32[48,128]{1,0:T(8,128)S(1)}, f32[48,128]{1,0:T(8,128)S(1)}, u32[]{:S(2)}, u32[]{:S(2)}) collective-permute-start(f32[48,128]{1,0:T(8,128)S(1)} %fusion.1), channel_id=1, source_target_pairs={{0,16},{8,24},{16,0},{24,8},{1,17},{9,25},{17,1},{25,9},{2,18},{10... | collective-permute-start | bytes 73736 | tf_op jit(solution)/shard_map/ppermute | solution.py:24

commit v6 on v5

--- a/solution.py
+++ b/solution.py
@@ -90,7 +90,7 @@
     lane_grp = (lane // ACC_BLK).astype(jnp.float32)
     later = jnp.where((lo_o == lane_acc) & (ki_o == lane_grp), wt_o, 0.0)
     pair_ref[...] = jnp.dot(
-        earlier_t, later, precision=lax.Precision.HIGHEST, preferred_element_type=jnp.float32
+        earlier_t, later, precision=lax.Precision.HIGH, preferred_element_type=jnp.float32
     )
     dirs = jnp.where(
         row == 0.0, jnp.where(ki_r < 2.5, wt_r, 0.0), jnp.where(row == 1.0, jnp.where(ki_r > 2.5, wt_r, 0.0), 0.0)
@@ -115,7 +115,7 @@
         trip_ref[b] = jnp.dot(
             ends[:, b * blk : (b + 1) * blk],
             last,
-            precision=lax.Precision.HIGHEST,
+            precision=lax.Precision.HIGH,
             preferred_element_type=jnp.float32,
         )
 

time: 47.2 us -> 46.9 us (level)
  no operation moved by 1% of the time
where the time goes in v6:
time: 46.9 us; the launch traced here: 46.5 us
  Pallas kernels  12.6 us (27%)
  blocking collectives  9.84 us (21%)
  starting transfers between devices  8.85 us (19%)
  local copies, waits for them, and re-layouts  7.05 us (15%)
  waiting for transfers between devices  5.03 us (11%)
  other arithmetic  2.38 us (5%)
  between operations  0.77 us (2%)
    pallas_call x1, Pallas kernels, count_blocks(): pl.pallas_call(motif_kernel, grid=(nb,), in_specs=[pl.BlockSpec((None, 8,...  12.6 us
    all_to_all x1, blocking collectives, per_device(): lax.all_to_all(stacked, 'dev', split_axis=0, concat_axis=3, tiled=True)[0]  9.84 us
    ppermute x2, starting transfers between devices, summed_over(): block = block + lax.ppermute(block, axis, [(i, i ^ step) for i in range(n)])  5.37 us
    ppermute x2, waiting for transfers between devices, summed_over(): block = block + lax.ppermute(block, axis, [(i, i ^ step) for i in range(n)])  3.61 us
    ppermute x1, starting transfers between devices, passed_along(): return lax.ppermute(block, axis, route)  3.48 us
    unnamed x14, local copies, waits for them, and re-layouts  2.65 us
    ppermute x1, waiting for transfers between devices, passed_along(): return lax.ppermute(block, axis, route)  1.41 us
    slice x2, local copies, waits for them, and re-layouts, per_device(): return (both[:36], both[40:])  1.2 us
  transfers between devices with their start and end apart: 3, of which 3 were waited for; matrix products, arithmetic and copies ran while one was open for 0% of the time, Pallas kernels for 0%

profile of v6, /device:TPU:0, one launch (start us, length us, event | category | flops | bytes accessed | tf_op | source)
XLA Modules:
  0.0 46.5 jit_solution(8024707693622972343)
XLA Ops:
  0.6 0.8 %reshape.81 = f32[8,8,1,32]{3,1,0,2:T(8,128)S(1)} reshape(bf16[2048]{0:T(1024)(128)(2,1)} %param.8) | data formatting | bytes 12288 | tf_op jit(solution)/shard_map/convert_element_type | solution.py:156
  1.4 0.5 %broadcast.22 = s32[]{:T(128)} broadcast(s32[]{:T(128)} %constant.23), dimensions={} | broadcast | bytes 8 | tf_op args[4]
  1.9 0.7 %reduce.3 = s32[64]{0:T(128)S(1)} reduce(s32[1,64]{1,0:T(1,128)S(1)} %copy-done.4, s32[]{:T(128)} %broadcast.22), dimensions={0}, to_apply=%param.9.reduce_sub_computation.3 | reduce | bytes 516 | tf_op args[4]
  2.6 0.1 gt.22
  2.8 0.6 %copy-done.2 = s32[2048]{0:T(1024)S(1)} copy-done((s32[2048]{0:T(1024)S(1)}, s32[2048]{0:T(1024)}, u32[]{:S(2)}) %copy-start.2) | copy-done | bytes 8216
  3.5 0.6 %copy-done.3 = s32[2048]{0:T(1024)S(1)} copy-done((s32[2048]{0:T(1024)S(1)}, s32[2048]{0:T(1024)}, u32[]{:S(2)}) %copy-start.3) | copy-done | bytes 8216
  4.2 0.1 reshape.91
  4.4 9.8 %all_to_all.15 = f32[8,1,1024]{2,1,0:T(1,128)S(1)} all-to-all(f32[8,1,1024]{2,1,0:T(1,128)S(1)} %reshape.91), channel_id=1, replica_groups=mesh['grp'=4,'dev'=8] {'dev'}, dimensions={0} | all-to-all | bytes 65536 | tf_op jit(solution)/shard_map/all_to_all | solution.py:166
  14.2 0.5 %broadcast.25 = f32[]{:T(128)} broadcast(f32[]{:T(128)} %constant.28), dimensions={} | broadcast | bytes 8 | tf_op jit(solution)/shard_map/all_to_all | solution.py:166
  14.7 0.7 %reduce.4 = f32[8,1024]{1,0:T(8,128)S(1)} reduce(f32[8,1,1024]{2,1,0:T(1,128)S(1)} %all_to_all.15, f32[]{:T(128)} %broadcast.25), dimensions={1}, to_apply=%all_to_all.11.reduce_sub_computation | reduce | bytes 65540 | tf_op jit(solution)/shard_map/all_to_all | solution.py:166
  15.5 0.1 reshape.92
  15.6 0.1 copy.18
  15.6 0.1 squeeze.3
  15.8 3.5 %collective-permute-start = (f32[8,4,256]{2,1,0:T(4,128)S(1)}, f32[8,4,256]{2,1,0:T(4,128)S(1)}, u32[]{:S(2)}, u32[]{:S(2)}) collective-permute-start(f32[8,4,256]{2,1,0:T(4,128)S(1)} %squeeze.3), channel_id=1, source_target_pairs={{0,8},{8,16},{16,24},{1,9},{9,17},{17,25},{2,10},{10,18},{18,26},{... | collective-permute-start | bytes 98312 | tf_op jit(solution)/shard_map/ppermute | solution.py:16
  19.3 0.1 pad.5.clone
  19.3 0.1 pad.1.clone
  19.4 1.4 %collective-permute-done = f32[8,4,256]{2,1,0:T(4,128)S(1)} collective-permute-done((f32[8,4,256]{2,1,0:T(4,128)S(1)}, f32[8,4,256]{2,1,0:T(4,128)S(1)}, u32[]{:S(2)}, u32[]{:S(2)}) %collective-permute-start) | collective-permute-done | bytes 32800 | tf_op jit(solution)/shard_map/ppermute | solution.py:16
  20.9 0.7 %maximum_maximum_fusion.r_ref = f32[8,8,512]{2,1,0:T(8,128)} fusion(f32[8,1,512]{2,1,0:T(1,128)S(1)} %slice_add_fusion, f32[8,4,512]{2,1,0:T(4,128)S(1)} %constant_dynamic-update-slice_fusion, f32[8]{0:T(128)S(1)} %pad.5.clone), kind=kLoop, calls=%fused_computation.1 | loop fusion | flops 65536 | bytes 213024 | tf_op jit(solution)/shard_map/concatenate | solution.py:127
  21.6 12.6 %shard_map.68 = (f32[8,8,128]{2,1,0:T(8,128)}, f32[8,2,8,128]{3,2,1,0:T(8,128)}) custom-call(f32[8,8,512]{2,1,0:T(8,128)} %maximum_maximum_fusion.r_ref), custom_call_target="tpu_custom_call" | custom-call | tf_op jit(solution)/shard_map/pallas_call | solution.py:128
  34.1 0.8 %slice.21 = f32[8,2,2,32]{3,2,1,0:T(2,128)S(1)} slice(f32[8,2,8,128]{3,2,1,0:T(8,128)} %get-tuple-element.5), slice={[0:8], [0:2], [0:2], [0:32]} | slice | bytes 8192 | tf_op jit(solution)/shard_map/slice | solution.py:145
  35.0 0.1 reshape.79
  35.1 0.1 reshape.80
  35.2 0.7 %copy-done = f32[8,8,128]{2,1,0:T(8,128)S(1)} copy-done((f32[8,8,128]{2,1,0:T(8,128)S(1)}, f32[8,8,128]{2,1,0:T(8,128)}, u32[]{:S(2)}) %copy-start) | copy-done | bytes 32792
  35.9 0.1 reshape.77
  36.0 0.1 reshape.78
  36.1 0.1 pad_maximum_fusion.1
  36.2 2.3 %collective-permute-start.1 = (f32[48,128]{1,0:T(8,128)S(1)}, f32[48,128]{1,0:T(8,128)S(1)}, u32[]{:S(2)}, u32[]{:S(2)}) collective-permute-start(f32[48,128]{1,0:T(8,128)S(1)} %pad_maximum_fusion.1), channel_id=1, source_target_pairs={{0,8},{8,0},{16,24},{24,16},{1,9},{9,1},{17,25},{25,17},{2,10},{10... | collective-permute-start | bytes 73736 | tf_op jit(solution)/shard_map/ppermute | solution.py:24
  38.5 1.8 %collective-permute-done.1 = f32[48,128]{1,0:T(8,128)S(1)} collective-permute-done((f32[48,128]{1,0:T(8,128)S(1)}, f32[48,128]{1,0:T(8,128)S(1)}, u32[]{:S(2)}, u32[]{:S(2)}) %collective-permute-start.1) | collective-permute-done | bytes 24608 | tf_op jit(solution)/shard_map/ppermute | solution.py:24
  40.4 3.0 %collective-permute-start.2 = (f32[48,128]{1,0:T(8,128)S(1)}, f32[48,128]{1,0:T(8,128)S(1)}, u32[]{:S(2)}, u32[]{:S(2)}) collective-permute-start(f32[48,128]{1,0:T(8,128)S(1)} %fusion.1), channel_id=1, source_target_pairs={{0,16},{8,24},{16,0},{24,8},{1,17},{9,25},{17,1},{25,9},{2,18},{10... | collective-permute-start | bytes 73736 | tf_op jit(solution)/shard_map/ppermute | solution.py:24
  43.5 1.8 %collective-permute-done.2 = f32[48,128]{1,0:T(8,128)S(1)} collective-permute-done((f32[48,128]{1,0:T(8,128)S(1)}, f32[48,128]{1,0:T(8,128)S(1)}, u32[]{:S(2)}, u32[]{:S(2)}) %collective-permute-start.2) | collective-permute-done | bytes 24608 | tf_op jit(solution)/shard_map/ppermute | solution.py:24
  45.3 0.6 %slice.26 = f32[36,128]{1,0:T(8,128)} slice(f32[48,128]{1,0:T(8,128)S(1)} %add.11), slice={[0:36], [0:128]} | slice | bytes 36864 | tf_op jit(solution)/shard_map/slice | solution.py:171
  45.9 0.6 %slice.27 = f32[8,128]{1,0:T(8,128)} slice(f32[48,128]{1,0:T(8,128)S(1)} %add.11), slice={[40:48], [0:128]} | slice | bytes 8192 | tf_op jit(solution)/shard_map/slice | solution.py:171
  (26 shorter events, 0.5 us)
Async XLA Ops:
  0.6 1.3 %copy-start.4 = (s32[1,64]{1,0:T(1,128)S(1)}, s32[1,64]{1,0:T(1,128)}, u32[]{:S(2)}) copy-start(s32[1,64]{1,0:T(1,128)} %param.9) | copy-start | bytes 772
  1.4 1.3 %copy-start.1 = (s32[2048]{0:T(1024)S(1)}, s32[2048]{0:T(1024)}, u32[]{:S(2)}) copy-start(s32[2048]{0:T(1024)} %param.7) | copy-start | bytes 24580
  2.7 0.7 %copy-start.2 = (s32[2048]{0:T(1024)S(1)}, s32[2048]{0:T(1024)}, u32[]{:S(2)}) copy-start(s32[2048]{0:T(1024)} %param.6) | copy-start | bytes 24580
  3.4 0.7 %copy-start.3 = (s32[2048]{0:T(1024)S(1)}, s32[2048]{0:T(1024)}, u32[]{:S(2)}) copy-start(s32[2048]{0:T(1024)} %param.5) | copy-start | bytes 24580
  15.8 5.1 %collective-permute-start = (f32[8,4,256]{2,1,0:T(4,128)S(1)}, f32[8,4,256]{2,1,0:T(4,128)S(1)}, u32[]{:S(2)}, u32[]{:S(2)}) collective-permute-start(f32[8,4,256]{2,1,0:T(4,128)S(1)} %squeeze.3), channel_id=1, source_target_pairs={{0,8},{8,16},{16,24},{1,9},{9,17},{17,25},{2,10},{10,18},{18,26},{... | collective-permute-start | bytes 98312 | tf_op jit(solution)/shard_map/ppermute | solution.py:16
  35.1 0.8 %copy-start = (f32[8,8,128]{2,1,0:T(8,128)S(1)}, f32[8,8,128]{2,1,0:T(8,128)}, u32[]{:S(2)}) copy-start(f32[8,8,128]{2,1,0:T(8,128)} %get-tuple-element.4) | copy-start | bytes 98308
  36.2 4.1 %collective-permute-start.1 = (f32[48,128]{1,0:T(8,128)S(1)}, f32[48,128]{1,0:T(8,128)S(1)}, u32[]{:S(2)}, u32[]{:S(2)}) collective-permute-start(f32[48,128]{1,0:T(8,128)S(1)} %pad_maximum_fusion.1), channel_id=1, source_target_pairs={{0,8},{8,0},{16,24},{24,16},{1,9},{9,1},{17,25},{25,17},{2,10},{10... | collective-permute-start | bytes 73736 | tf_op jit(solution)/shard_map/ppermute | solution.py:24
  40.4 4.8 %collective-permute-start.2 = (f32[48,128]{1,0:T(8,128)S(1)}, f32[48,128]{1,0:T(8,128)S(1)}, u32[]{:S(2)}, u32[]{:S(2)}) collective-permute-start(f32[48,128]{1,0:T(8,128)S(1)} %fusion.1), channel_id=1, source_target_pairs={{0,16},{8,24},{16,0},{24,8},{1,17},{9,25},{17,1},{25,9},{2,18},{10... | collective-permute-start | bytes 73736 | tf_op jit(solution)/shard_map/ppermute | solution.py:24
